TPU v7x, 128 devices: a whole 4x4x4 slice. The times are simulated.
128 devices in a mesh: row: 16 (over x, z), col: 8 (over y, core).
Axes of the slice: x: 4, y: 4, z: 4, core: 2. Of those that a mesh axis runs over, the one named last changes fastest.
Arguments:
- prior_covariance: float32 [16384, 16384], P('row', 'col'), may hold values from -1 to 12, as said below
- vel_first: float32 [128, 128], replicated, may hold values from -0.25 to 0.25
- vel_second: float32 [128, 128], replicated, may hold values from -0.25 to 0.25
- obs_cell: int32 [512, 2], replicated, may hold values from 0 to 126, as said below
- obs_noise: float32 [512], replicated, may hold values from 0.1 to 1
Outputs:
- analysis_covariance: float32 [16384, 16384], P('row', 'col')
Inputs may be any that keep to these rules, and one draw needn't show every extreme that they name: `prior_covariance`: symmetric and positive definite. Observation o interpolates the cells (i, j), (i, j + 1), (i + 1, j), (i + 1, j + 1) with i = obs_cell[o, 0] and j = obs_cell[o, 1].
All inputs are finite; a program needn't handle non-finite values.
Results may differ from a plain program's by a relative error of at most 0.000065.
Values sent between devices are 32-bit elements; how exact they have to be, the bound alone decides.
A program may use at most 192 MiB of HBM per device.

v0:
```python
import jax
import jax.numpy as jnp
from jax import lax
from jax.sharding import PartitionSpec as P

dispersion = 0.125
centre_weight = 1.0 - 4.0 * dispersion
interp_weights = (0.42, 0.28, 0.18, 0.12)
finest_accuracy = lax.Precision.HIGHEST


def extended_2(block, sides, width):
    for axis, dim in sides:
        count = lax.axis_size(axis)
        forward = [(i, i + 1) for i in range(count - 1)]
        backward = [(target, source) for source, target in forward]
        low = lax.ppermute(
            lax.slice_in_dim(block, block.shape[dim] - width, None, axis=dim), axis, forward
        )
        high = lax.ppermute(lax.slice_in_dim(block, 0, width, axis=dim), axis, backward)
        block = jnp.concatenate([low, block, high], axis=dim)
    return block


def stencil_weights(vel_first, vel_second, line_start, line_count):
    first_rows = lax.dynamic_slice_in_dim(vel_first, line_start, line_count, 0)
    second_rows = lax.dynamic_slice_in_dim(vel_second, line_start, line_count, 0)
    return (
        dispersion - 0.5 * first_rows,
        dispersion + 0.5 * first_rows,
        dispersion - 0.5 * second_rows,
        dispersion + 0.5 * second_rows,
    )


def sweep_rows(extended, weights, line_count, neighbour_cells):
    span_cols = extended.shape[1]
    slab_view = extended.reshape(line_count + 2, neighbour_cells, span_cols)
    middle = slab_view[1:-1]
    zero_edge = jnp.zeros((line_count, 1, span_cols), jnp.float32)
    next_second = jnp.concatenate([middle[:, 1:], zero_edge], axis=1)
    prev_second = jnp.concatenate([zero_edge, middle[:, :-1]], axis=1)
    toward_next, toward_prev, across_next, across_prev = [
        weight_field[:, :, None] for weight_field in weights
    ]
    result = (
        centre_weight * middle
        + toward_next * slab_view[2:]
        + toward_prev * slab_view[:-2]
        + across_next * next_second
        + across_prev * prev_second
    )
    return result.reshape(line_count * neighbour_cells, span_cols)


def traverse_verticals(extended, weights, line_count, neighbour_cells):
    span_rows = extended.shape[0]
    slab_view = extended.reshape(span_rows, line_count + 2, neighbour_cells)
    middle = slab_view[:, 1:-1]
    zero_edge = jnp.zeros((span_rows, line_count, 1), jnp.float32)
    next_second = jnp.concatenate([middle[:, :, 1:], zero_edge], axis=2)
    prev_second = jnp.concatenate([zero_edge, middle[:, :, :-1]], axis=2)
    toward_next, toward_prev, across_next, across_prev = [
        weight_field[None] for weight_field in weights
    ]
    result = (
        centre_weight * middle
        + toward_next * slab_view[:, 2:]
        + toward_prev * slab_view[:, :-2]
        + across_next * next_second
        + across_prev * prev_second
    )
    return result.reshape(span_rows, line_count * neighbour_cells)


def body(prior_covariance, vel_first, vel_second, obs_cell, obs_noise):
    local_rows, local_columns = prior_covariance.shape
    neighbour_cells = vel_first.shape[0]
    observation_count = obs_noise.shape[0]
    row_lines = local_rows // neighbour_cells
    column_lines = local_columns // neighbour_cells
    row_place = lax.axis_index("row")
    col_place = lax.axis_index("col")
    left_weights = stencil_weights(vel_first, vel_second, row_place * row_lines, row_lines)
    right_stencil_weights = stencil_weights(
        vel_first, vel_second, col_place * column_lines, column_lines
    )
    extended = extended_2(prior_covariance, (("row", 0),), neighbour_cells)
    propagated_covariance = sweep_rows(extended, left_weights, row_lines, neighbour_cells)
    propagated_covariance = extended_2(propagated_covariance, (("col", 1),), neighbour_cells)
    prior_mean_vector = traverse_verticals(
        propagated_covariance, right_stencil_weights, column_lines, neighbour_cells
    )
    corner = obs_cell[:, 0] * neighbour_cells + obs_cell[:, 1]
    measured_sites = jnp.stack(
        [corner, corner + 1, corner + neighbour_cells, corner + neighbour_cells + 1]
    )
    interp = jnp.array(interp_weights, jnp.float32)[:, None]
    row_offset = measured_sites - row_place * local_rows
    row_coeffs = jnp.where((row_offset >= 0) & (row_offset < local_rows), interp, 0.0)
    horizontal_slot = jnp.clip(row_offset, 0, local_rows - 1).reshape(-1)
    col_offset = measured_sites - col_place * local_columns
    col_coeffs = jnp.where((col_offset >= 0) & (col_offset < local_columns), interp, 0.0)
    vertical_slot = jnp.clip(col_offset, 0, local_columns - 1).reshape(-1)
    chosen_entries = jnp.take(prior_mean_vector, vertical_slot, axis=1).reshape(
        local_rows, 4, observation_count
    )
    gain_part = jnp.sum(chosen_entries * col_coeffs[None], axis=1)
    gain_rows = lax.psum(gain_part, "col")
    gathered_entries = jnp.take(prior_mean_vector, horizontal_slot, axis=0).reshape(
        4, observation_count, local_columns
    )
    observed = jnp.sum(gathered_entries * row_coeffs[:, :, None], axis=0)
    rows_pick = jnp.take(gain_rows, horizontal_slot, axis=0).reshape(
        4, observation_count, observation_count
    )
    innov_part = jnp.sum(rows_pick * row_coeffs[:, :, None], axis=0)
    innov_total = lax.psum(innov_part, "row")
    innovation = innov_total + jnp.diag(obs_noise)
    symmetric = 0.5 * (innovation + innovation.T)
    factor = jnp.linalg.cholesky(symmetric)
    inverse = jax.scipy.linalg.solve_triangular(
        factor, jnp.eye(observation_count, dtype=jnp.float32), lower=True
    )
    update_rows = jnp.dot(
        gain_rows, inverse.T, precision=finest_accuracy, preferred_element_type=jnp.float32
    )
    observed_cols = lax.psum(observed, "row")
    update_cols = jnp.dot(
        inverse, observed_cols, precision=finest_accuracy, preferred_element_type=jnp.float32
    )
    mean_increment = jnp.dot(
        update_rows, update_cols, precision=finest_accuracy, preferred_element_type=jnp.float32
    )
    return prior_mean_vector - mean_increment


def solution(mesh):
    placed = (P("row", "col"), P(), P(), P(), P())
    return jax.shard_map(
        body, mesh=mesh, in_specs=placed, out_specs=P("row", "col"), check_vma=False
    )
```

profile of v0, /device:TPU:1, one launch (start us, length us, event | category | flops | bytes accessed | tf_op | source)
XLA Modules:
  0.0 542.0 jit_solution(2982019623615949212)
XLA Ops:
  9.5 6.0 %collective-permute-start.1 = (f32[128,2048]{1,0:T(8,128)S(1)}, f32[128,2048]{1,0:T(8,128)}, u32[]{:S(2)}, u32[]{:S(2)}) collective-permute-start(f32[128,2048]{1,0:T(8,128)S(1)} %get-tuple-element.46), channel_id=1, source_target_pairs={{0,8},{8,16},{16,24},{24,32},{32,40},{40,48},{48,56},{56,64},{64,7... | collective-permute-start | bytes 3145736 | tf_op jit(solution)/shard_map/ppermute | solution.py:17
  15.5 9.3 %copy.35 = f32[8,128,2048]{1,0,2:T(8,128)} copy(f32[8,128,2048]{2,1,0:T(8,128)} %bitcast.94) | data formatting | bytes 16777216 | tf_op jit(solution)/shard_map/slice | solution.py:39
  26.4 12.8 %fusion.52 = (f32[8,127,2048]{1,0,2:T(8,128)}, f32[8,127,2048]{1,0,2:T(8,128)}) fusion(f32[8,128,2048]{1,0,2:T(8,128)} %copy.35), kind=kLoop, calls=%fused_computation.127 | loop fusion | bytes 33292288 | tf_op jit(solution)/shard_map/slice | solution.py:41
  39.2 10.8 %pad_maximum_fusion.2 = (f32[1024,2048]{1,0:T(8,128)}, f32[1024,2048]{1,0:T(8,128)}) fusion(f32[128,2048]{1,0:T(8,128)S(1)} %collective-permute-done, f32[1024,2048]{1,0:T(8,128)} %param.6, f32[128,2048]{1,0:T(8,128)} %collective-permute-done.1), kind=kLoop, calls=%fused_computation.16 | loop fusion | flops 4194304 | bytes 27262976 | tf_op jit(solution)/shard_map/concatenate | solution.py:21
  50.1 9.3 %copy.36 = f32[8,128,2048]{1,0,2:T(8,128)} copy(f32[8,128,2048]{2,1,0:T(8,128)} %bitcast.99) | data formatting | bytes 16777216 | tf_op jit(solution)/shard_map/slice | solution.py:48
  59.4 9.3 %copy.37 = f32[8,128,2048]{1,0,2:T(8,128)} copy(f32[8,128,2048]{2,1,0:T(8,128)} %bitcast.98) | data formatting | bytes 16777216 | tf_op jit(solution)/shard_map/slice | solution.py:49
  68.6 18.2 %multiply_add_fusion = f32[8,128,2048]{1,0,2:T(8,128)} fusion(f32[8,127,2048]{1,0,2:T(8,128)} %get-tuple-element.48, f32[8,127,2048]{1,0,2:T(8,128)} %get-tuple-element.47, f32[8,128,2048]{1,0,2:T(8,128)} %copy.37, f32[8,128,2048]{1,0,2:T(8,128)} %copy.36, f32[8,128,2048]{1,0,2:T(8,128)} %copy.35, f32[8,128]{1,0:T(8,128)S(1)} %get-tuple-element.71, ...), kind=kLoop, calls=%fused_computation.18 | loop fusion | flops 18874368 | bytes 50216960 | tf_op jit(solution)/shard_map/add | solution.py:47
  86.8 5.5 %copy.68 = f32[256,8,8,128]{3,1,2,0:T(8,128)S(1)} copy(f32[256,8,8,128]{3,2,1,0:T(8,128)} %bitcast.100) | data formatting | bytes 16777216
  95.8 4.1 collective-permute-start.2
  106.1 4.4 collective-permute-done.3
  110.5 8.9 %pad_maximum_fusion = f32[1024,2304]{0,1:T(8,128)} fusion(f32[1024,128]{0,1:T(8,128)S(1)} %collective-permute-done.3, f32[1024,2048]{0,1:T(8,128)} %bitcast.96, f32[1024,128]{0,1:T(8,128)S(1)} %collective-permute-done.2), kind=kLoop, calls=%fused_computation.6 | loop fusion | flops 4718592 | bytes 18874368 | tf_op jit(solution)/shard_map/concatenate | solution.py:21
  119.4 10.7 %fusion.49 = (f32[1024,16,127]{0,2,1:T(8,128)S(1)}, f32[1024,16,127]{0,2,1:T(8,128)}) fusion(f32[1024,18,128]{0,2,1:T(8,128)} %bitcast.89), kind=kLoop, calls=%fused_computation.124 | loop fusion | bytes 33292288 | tf_op jit(solution)/shard_map/slice | solution.py:61
  130.1 9.2 %fusion.2 = f32[1024,16,128]{0,2,1:T(8,128)} fusion(f32[1024,18,128]{0,2,1:T(8,128)S(1)} %bitcast.92, f32[1024,16,127]{0,2,1:T(8,128)} %get-tuple-element.40, f32[1024,16,127]{0,2,1:T(8,128)S(1)} %get-tuple-element.39, f32[16,128]{1,0:T(8,128)S(1)} %get-tuple-element.73, f32[16,128]{1,0:T(8,128)S(1)} %get-tuple-element.74, ...), kind=kLoop, calls=%fused_computation.11 | loop fusion | flops 18874368 | bytes 50233344 | tf_op jit(solution)/shard_map/add | solution.py:67
  139.4 15.0 %gather_fusion = f32[2048,1024]{1,0:T(8,128)} fusion(f32[1024,2048]{0,1:T(8,128)} %bitcast.87, s32[2048]{0:T(1024)S(1)} %broadcast_clamp_fusion.1), kind=kCustom, calls=%fused_computation | custom fusion | bytes 16785408 | tf_op jit(solution)/shard_map/jit(_take)/gather | solution.py:105
  154.4 4.1 multiply_reduce_fusion.1
  160.4 9.1 %copy.62 = f32[1024,2048]{1,0:T(8,128)} copy(f32[1024,2048]{0,1:T(8,128)} %bitcast.88) | data formatting | bytes 16777216 | tf_op jit(solution)/shard_map/reshape | solution.py:73
  169.6 20.1 %gather_fusion.2 = f32[2048,2048]{1,0:T(8,128)} fusion(f32[1024,2048]{1,0:T(8,128)} %copy.62, s32[2048]{0:T(1024)S(1)} %broadcast_clamp_fusion), kind=kCustom, calls=%fused_computation.2 | custom fusion | bytes 33562624 | tf_op jit(solution)/shard_map/jit(_take)/gather | solution.py:110
  189.7 9.3 %multiply_reduce_fusion = f32[512,2048]{1,0:T(8,128)} fusion(f32[4,512,2048]{2,1,0:T(8,128)} %bitcast.93, f32[4,512]{1,0:T(4,128)S(1)} %get-tuple-element.63, pred[4,512]{1,0:T(4,128)(4,1)S(1)} %get-tuple-element.65), kind=kLoop, calls=%fused_computation.5 | loop fusion | flops 11534336 | bytes 20981760 | tf_op jit(solution)/shard_map/reduce_sum | solution.py:113
  199.0 28.1 %all-reduce.9.cloned.1.call-done = f32[1024,512]{1,0:T(8,128)} async-done(((f32[1024,512]{1,0:T(8,128)}), f32[1024,512]{1,0:T(8,128)}) %all-reduce.9.cloned.1.call-update) | async-done | bytes 2097168 | tf_op jit(solution)/shard_map/psum | solution.py:109
  227.1 11.1 %gather_fusion.1 = f32[2048,512]{1,0:T(8,128)} fusion(f32[1024,512]{1,0:T(8,128)} %all-reduce.9.cloned.1.call-done, s32[2048]{0:T(1024)S(1)} %broadcast_clamp_fusion), kind=kCustom, calls=%fused_computation.1 | custom fusion | bytes 8396800 | tf_op jit(solution)/shard_map/jit(_take)/gather | solution.py:114
  242.8 114.2 %all-reduce.11.cloned.1.call-done = (f32[512,512]{0,1:T(8,128)}, f32[512,2048]{1,0:T(8,128)}) async-done(((f32[512,512]{0,1:T(8,128)}, f32[512,2048]{1,0:T(8,128)}), (f32[512,512]{0,1:T(8,128)}, f32[512,2048]{1,0:T(8,128)})) %all-reduce.11.cloned.1.call-update) | async-done | bytes 5242896 | tf_op jit(solution)/shard_map/psum | solution.py:118
  361.7 11.7 %cholesky.103 = f32[128,128]{1,0:T(8,128)S(1)} custom-call(f32[128,128]{1,0:T(8,128)S(1)} %cholesky.263), custom_call_target="Cholesky" | custom-call | tf_op jit(solution)/shard_map/jit(cholesky)/cholesky | solution.py:121
  373.4 9.8 %custom-call.31 = f32[1,128,128]{1,2,0:T(8,128)S(1)} custom-call(f32[1,128,128]{2,1,0:T(8,128)S(1)} %get-tuple-element.54), custom_call_target="InvertDiagBlocksLowerTriangular" | custom-call | tf_op jit(solution)/shard_map/jit(cholesky)/cholesky | solution.py:121
  385.8 11.7 %cholesky.215 = f32[128,128]{1,0:T(8,128)S(1)} custom-call(f32[128,128]{1,0:T(8,128)S(1)} %cholesky.267), custom_call_target="Cholesky" | custom-call | tf_op jit(solution)/shard_map/jit(cholesky)/cholesky | solution.py:121
  398.0 9.8 %custom-call.32 = f32[1,128,128]{1,2,0:T(8,128)S(1)} custom-call(f32[1,128,128]{2,1,0:T(8,128)S(1)} %get-tuple-element.52), custom_call_target="InvertDiagBlocksLowerTriangular" | custom-call | tf_op jit(solution)/shard_map/jit(cholesky)/cholesky | solution.py:121
  409.8 11.7 %cholesky.236 = f32[128,128]{1,0:T(8,128)S(1)} custom-call(f32[128,128]{1,0:T(8,128)S(1)} %cholesky.272), custom_call_target="Cholesky" | custom-call | tf_op jit(solution)/shard_map/jit(cholesky)/cholesky | solution.py:121
  421.7 9.8 %custom-call.33 = f32[1,128,128]{1,2,0:T(8,128)S(1)} custom-call(f32[1,128,128]{2,1,0:T(8,128)S(1)} %get-tuple-element.50), custom_call_target="InvertDiagBlocksLowerTriangular" | custom-call | tf_op jit(solution)/shard_map/jit(cholesky)/cholesky | solution.py:121
  433.1 11.9 %cholesky.253 = f32[128,128]{1,0:T(8,128)S(1)} custom-call(f32[128,128]{1,0:T(8,128)S(1)} %convolution_subtract_fusion.6), custom_call_target="Cholesky" | custom-call | tf_op jit(solution)/shard_map/jit(cholesky)/cholesky | solution.py:121
  450.3 10.7 %while.1 = (s32[]{:T(128)}, f32[512,512]{0,1:T(8,128)S(1)}, s32[4,2]{0,1:T(2,128)S(1)}, f32[4,128,128]{2,1,0:T(8,128)}, s32[]{:T(128)}) while((s32[]{:T(128)}, f32[512,512]{0,1:T(8,128)S(1)}, s32[4,2]{0,1:T(2,128)S(1)}, f32[4,128,128]{2,1,0:T(8,128)}, s32[]{:T(128)}) %tuple.43), condition=%wide.while_cond, body=%wide.while_body.sunk | while | flops 2 | bytes 393829 | solution.py:122
  461.0 40.1 %custom-call.34 = f32[4,128,128]{1,2,0:T(8,128)S(1)} custom-call(f32[4,128,128]{2,1,0:T(8,128)} %get-tuple-element.12), custom_call_target="InvertDiagBlocksLowerTriangular" | custom-call | tf_op jit(solution)/shard_map/jit(_solve_triangular)/triangular_solve | solution.py:122
  505.8 9.2 %fusion.11 = f32[512,2048]{1,0:T(8,128)S(1)} fusion(f32[512,2048]{1,0:T(8,128)} %get-tuple-element.34, f32[128,512]{1,0:T(8,128)S(1)} %fusion.27, f32[128,512]{1,0:T(8,128)S(1)} %fusion.28, f32[128,512]{1,0:T(8,128)S(1)} %fusion.30, f32[128,512]{1,0:T(8,128)S(1)} %fusion.18), kind=kOutput, calls=%fused_computation.43 | convolution fusion | flops 6443237376 | bytes 9437184 | tf_op jit(solution)/shard_map/dot_general | solution.py:129
  518.6 16.1 %convolution_subtract_fusion = f32[1024,2048]{1,0:T(8,128)} fusion(f32[1024,2048]{1,0:T(8,128)S(1)} %bitcast.86, f32[1024,512]{1,0:T(8,128)S(1)} %fusion.12, f32[512,2048]{1,0:T(8,128)S(1)} %fusion.11), kind=kOutput, calls=%fused_computation.20 | convolution fusion | flops 12886999040 | bytes 23068672 | tf_op jit(solution)/shard_map/dot_general | solution.py:132
  (117 shorter events, 53.7 us)
Async XLA Ops:
  6.5 220.6 %all-reduce.9.cloned.1.call-start = ((), (), s32[]{:S(2)}) async-start(), calls=%async_computation | async-start | bytes 4194304 | tf_op jit(solution)/shard_map/psum | solution.py:109
  8.2 31.0 %collective-permute-start = (f32[128,2048]{1,0:T(8,128)S(1)}, f32[128,2048]{1,0:T(8,128)S(1)}, u32[]{:S(2)}, u32[]{:S(2)}) collective-permute-start(f32[128,2048]{1,0:T(8,128)S(1)} %get-tuple-element.45), channel_id=1, source_target_pairs={{8,0},{16,8},{24,16},{32,24},{40,32},{48,40},{56,48},{64,56},{72,6... | collective-permute-start | bytes 3145736 | tf_op jit(solution)/shard_map/ppermute | solution.py:20
  9.5 29.7 %collective-permute-start.1 = (f32[128,2048]{1,0:T(8,128)S(1)}, f32[128,2048]{1,0:T(8,128)}, u32[]{:S(2)}, u32[]{:S(2)}) collective-permute-start(f32[128,2048]{1,0:T(8,128)S(1)} %get-tuple-element.46), channel_id=1, source_target_pairs={{0,8},{8,16},{16,24},{24,32},{32,40},{40,48},{48,56},{56,64},{64,7... | collective-permute-start | bytes 3145736 | tf_op jit(solution)/shard_map/ppermute | solution.py:17
  15.5 10.7 %copy-start.4 = (s32[512,2]{0,1:T(2,128)S(1)}, s32[512,2]{0,1:T(2,128)}, u32[]{:S(2)}) copy-start(s32[512,2]{0,1:T(2,128)} %param.9) | copy-start | bytes 12292
  15.5 10.8 %copy-start.5 = (f32[4]{0:T(128)S(1)}, f32[4]{0:T(128)}, u32[]{:S(2)}) copy-start(f32[4]{0:T(128)} %constant.228.clone) | copy-start | bytes 52
  92.3 3.4 copy-start.1
  95.8 10.3 %collective-permute-start.2 = (f32[1024,128]{0,1:T(8,128)S(1)}, f32[1024,128]{0,1:T(8,128)S(1)}, u32[]{:S(2)}, u32[]{:S(2)}) collective-permute-start(f32[1024,128]{0,1:T(8,128)S(1)} %get-tuple-element.41), channel_id=1, source_target_pairs={{0,1},{1,2},{2,3},{3,4},{4,5},{5,6},{6,7},{8,9},{9,10},{10,11},{11... | collective-permute-start | bytes 1572872 | tf_op jit(solution)/shard_map/ppermute | solution.py:17
  100.0 10.5 %collective-permute-start.3 = (f32[1024,128]{0,1:T(8,128)S(1)}, f32[1024,128]{0,1:T(8,128)S(1)}, u32[]{:S(2)}, u32[]{:S(2)}) collective-permute-start(f32[1024,128]{0,1:T(8,128)S(1)} %get-tuple-element.42), channel_id=1, source_target_pairs={{1,0},{2,1},{3,2},{4,3},{5,4},{6,5},{7,6},{9,8},{10,9},{11,10},{12... | collective-permute-start | bytes 1572872 | tf_op jit(solution)/shard_map/ppermute | solution.py:20
  119.4 10.7 %slice-start.2 = ((s8[9437184]{0:T(1024)(128)(4,1)}), s8[4194304]{0:T(1024)(128)(4,1)S(1)}, s32[]{:S(2)}) async-start(s8[9437184]{0:T(1024)(128)(4,1)} %bitcast.90), calls=%async_computation.4 | async-start | bytes 8388608
  119.4 10.7 %slice-start.3 = ((s8[9437184]{0:T(1024)(128)(4,1)}), s8[4194304]{0:T(1024)(128)(4,1)S(1)}, s32[]{:S(2)}) async-start(s8[9437184]{0:T(1024)(128)(4,1)} %bitcast.90), calls=%async_computation.5 | async-start | bytes 8388608
  119.4 10.8 %slice-start.4 = ((s8[9437184]{0:T(1024)(128)(4,1)}), s8[1048576]{0:T(1024)(128)(4,1)S(1)}, s32[]{:S(2)}) async-start(s8[9437184]{0:T(1024)(128)(4,1)} %bitcast.90), calls=%async_computation.6 | async-start | bytes 2097152
  160.4 196.6 %all-reduce.11.cloned.1.call-start = ((), (), s32[]{:S(2)}) async-start(), calls=%async_computation.1 | async-start | bytes 10485760 | tf_op jit(solution)/shard_map/psum | solution.py:118
  238.2 118.8 %copy-start.3 = (f32[512]{0:T(512)S(1)}, f32[512]{0:T(512)}, u32[]{:S(2)}) copy-start(f32[512]{0:T(512)} %param.10) | copy-start | bytes 6148
  360.7 1.0 copy-start.2
  501.4 13.6 %copy-start = (f32[1024,512]{1,0:T(8,128)S(1)}, f32[1024,512]{1,0:T(8,128)}, u32[]{:S(2)}) copy-start(f32[1024,512]{1,0:T(8,128)} %all-reduce.9.cloned.1.call-done) | copy-start | bytes 6291460
  505.8 12.8 %slice-start = ((s8[8388608]{0:T(1024)(128)(4,1)}), s8[4194304]{0:T(1024)(128)(4,1)S(1)}, s32[]{:S(2)}) async-start(s8[8388608]{0:T(1024)(128)(4,1)} %bitcast.85), calls=%async_computation.2 | async-start | bytes 8388608
  505.8 12.7 %slice-start.1 = ((s8[8388608]{0:T(1024)(128)(4,1)}), s8[4194304]{0:T(1024)(128)(4,1)S(1)}, s32[]{:S(2)}) async-start(s8[8388608]{0:T(1024)(128)(4,1)} %bitcast.85), calls=%async_computation.3 | async-start | bytes 8388608
Sparse Core Ops, SparseCore 0:
  160.5 66.5 all-reduce.8
  242.7 114.2 all-reduce.10
where the time goes:
time: 550 us; the launch traced here: 542 us
  other arithmetic  188 us (34%)
  waiting for transfers between devices  151 us (27%)
  local copies, waits for them, and re-layouts  134 us (24%)
  matrix products  39.4 us (7%)
  between operations  16.8 us (3%)
  starting transfers between devices  13.6 us (2%)
    psum x1, waiting for transfers between devices, body(): innov_total = lax.psum(innov_part, 'row')  114 us
    another operation x15, other arithmetic, body(): factor = jnp.linalg.cholesky(symmetric)  79.2 us
    another operation x3, other arithmetic, body(): jax.scipy.linalg.solve_triangular(factor, jnp.eye(observation_count, dtyp...  40.3 us
    psum x1, waiting for transfers between devices, body(): gain_rows = lax.psum(gain_part, 'col')  28.1 us
    gather x1, local copies, waits for them, and re-layouts, body(): jnp.take(prior_mean_vector, horizontal_slot, axis=0)  20.1 us
    concatenate x2, other arithmetic, extended_2(): block = jnp.concatenate([low, block, high], axis=dim)  19.7 us
    add x1, other arithmetic, sweep_rows(): centre_weight * middle + toward_next * slab_view[2:]  18.2 us
    dot_general x1, matrix products, body(): jnp.dot(update_rows, update_cols, precision=finest_accuracy, preferred_el...  16.1 us
  transfers between devices with their start and end apart: 6, of which 4 were waited for; matrix products, arithmetic and copies ran while one was open for 12% of the time, Pallas kernels for 0%

commit v1 on v0

v1 whole, which is shorter than its diff:
```python
import functools
import jax
import jax.numpy as jnp
from jax import lax
from jax.experimental import pallas as pl
from jax.experimental.pallas import tpu as pltpu
from jax.sharding import PartitionSpec as P

HI = lax.Precision.HIGHEST
F32, BF16 = jnp.float32, jnp.bfloat16
dispersion = 0.125
centre_weight = 1.0 - 4.0 * dispersion
interp_weights = (0.42, 0.28, 0.18, 0.12)

def split(x):
    hi = x.astype(BF16)
    return hi, (x - hi.astype(F32)).astype(BF16)

def dot3(a, b, dims):
    (ah, al), (bh, bl) = a, b
    dg = functools.partial(lax.dot_general, dimension_numbers=(dims, ((), ())), preferred_element_type=F32)
    return dg(ah, bh) + (dg(ah, bl) + dg(al, bh))

def observed_weights(velf_ref, vels_ref, oi, oj):
    cells, count = velf_ref.shape[0], oi.shape[1]
    cid = lax.broadcasted_iota(jnp.int32, (cells, count), 0)
    w = {}
    def add(di, dj, v):
        w[di, dj] = w[di, dj] + v if (di, dj) in w else v
    for a in (0, 1):
        pick = jnp.where(cid == oi + a, 1.0, 0.0).astype(F32)
        by_j = [lax.dot_general(v[...], pick, (((0,), (0,)), ((), ())), precision=HI, preferred_element_type=F32)
                for v in (velf_ref, vels_ref)]
        for b in (0, 1):
            here = cid == oj + b
            vf, vs = [jnp.sum(jnp.where(here, x, 0.0), axis=0, keepdims=True) for x in by_j]
            h = interp_weights[2 * a + b]
            add(a, b, jnp.full_like(vf, h * centre_weight))
            add(a + 1, b, h * (dispersion - 0.5 * vf))
            add(a - 1, b, h * (dispersion + 0.5 * vf))
            add(a, b + 1, h * (dispersion - 0.5 * vs))
            add(a, b - 1, h * (dispersion + 0.5 * vs))
    return w

def line_weights(w, oi, oj, line, cells):
    count = oi.shape[1]
    jid = lax.broadcasted_iota(jnp.int32, (cells, count), 0)
    out = jnp.zeros((cells, count), F32)
    for dj in (-1, 0, 1, 2):
        row = jnp.zeros((1, count), F32)
        for di in (-1, 0, 1, 2):
            if (di, dj) in w:
                row = row + jnp.where(oi + di == line, w[di, dj], 0.0)
        out = jnp.where(jid == oj + dj, row, out)
    return out

def t_kernel(place_ref, p_hbm, velf_ref, vels_ref, oi_ref, oj_ref, t_ref, s_ref, buf, ch, cl, wsc, sems, *, tile):
    rows, cols = p_hbm.shape
    cells = velf_ref.shape[0]
    steps = rows // tile
    def fetch(n):
        return pltpu.make_async_copy(p_hbm.at[pl.ds(n * tile, tile), :], buf.at[n], sems.at[n])
    for n in range(steps):
        fetch(n).start()
    oi, oj = oi_ref[...], oj_ref[...]
    w = observed_weights(velf_ref, vels_ref, oi, oj)
    first_row, first_col = place_ref[0], place_ref[1]
    keys = sorted(w)
    for n, key in enumerate(keys):
        wsc[n:n + 1, :] = w[key]
    def build(l, _):
        ww = {key: wsc[n:n + 1, :] for n, key in enumerate(keys)}
        hi, lo = split(line_weights(ww, oi_ref[...], oj_ref[...], first_col + l, cells))
        at = pl.multiple_of(l * cells, cells)
        ch[pl.ds(at, cells), :] = hi
        cl[pl.ds(at, cells), :] = lo
        return 0
    lax.fori_loop(0, cols // cells, build, 0)
    s_ref[...] = jnp.zeros_like(s_ref)
    lines = tile // cells
    def run(n, _):
        pltpu.make_async_copy(p_hbm.at[pl.ds(n * tile, tile), :], buf.at[n], sems.at[n]).wait()
        t = dot3(split(buf[n]), (ch[...], cl[...]), ((1,), (0,)))
        t_ref[pl.ds(pl.multiple_of(n * tile, tile), tile), :] = t
        ww = {key: wsc[m:m + 1, :] for m, key in enumerate(keys)}
        c = jnp.concatenate([line_weights(ww, oi_ref[...], oj_ref[...], first_row + n * lines + m, cells)
                             for m in range(lines)], axis=0)
        s_ref[...] += dot3(split(c), split(t), ((0,), (0,)))
        return 0
    lax.fori_loop(0, steps, run, 0)

def partials(place, p, velf, vels, oi, oj, tile=256):
    rows, cols = p.shape
    count = oi.shape[1]
    v = pl.BlockSpec(memory_space=pltpu.VMEM)
    return pl.pallas_call(functools.partial(t_kernel, tile=tile),
        out_shape=(jax.ShapeDtypeStruct((rows, count), F32), jax.ShapeDtypeStruct((count, count), F32)),
        in_specs=[pl.BlockSpec(memory_space=pltpu.SMEM), pl.BlockSpec(memory_space=pl.ANY), v, v, v, v],
        out_specs=(v, v),
        scratch_shapes=[pltpu.VMEM((rows // tile, tile, cols), F32), pltpu.VMEM((cols, count), BF16),
                        pltpu.VMEM((cols, count), BF16), pltpu.VMEM((16, count), F32),
                        pltpu.SemaphoreType.DMA((rows // tile,))],
        compiler_params=pltpu.CompilerParams(vmem_limit_bytes=60 << 20),
        cost_estimate=pl.CostEstimate(flops=8 * 10**9, bytes_accessed=12 << 20, transcendentals=0),
    )(place, p, velf, vels, oi, oj)


def left_sweep(prev, mid, nxt, w):
    cells = mid.shape[0]
    up = pltpu.roll(mid, cells - 1, 0)
    down = pltpu.roll(mid, 1, 0)
    return centre_weight * mid + w[0] * nxt + w[1] * prev + w[2] * up + w[3] * down

def f_kernel(wl_ref, wr_ref, top_ref, p_prev, p_mid, p_next, bot_ref, lo_ref, hi_ref, f_ref, q_ref):
    n = pl.program_id(0)
    last = pl.num_programs(0) - 1
    cells = p_mid.shape[0]
    cols = p_mid.shape[1]
    lines = cols // cells
    at = pl.multiple_of(n * cells, cells)
    wide = [jnp.broadcast_to(wl_ref[:, m:m + 1], (cells, cells)) for m in range(4)]
    def side(ref):
        return [ref[pl.ds(at + d * cells, cells), :] for d in (0, 1, 2)]
    q_ref[:, 0:cells] = left_sweep(*side(lo_ref), wide)
    q_ref[:, (lines + 1) * cells:] = left_sweep(*side(hi_ref), wide)
    for l in range(lines):
        s = slice(l * cells, (l + 1) * cells)
        prev = jnp.where(n == 0, top_ref[:, s], p_prev[:, s])
        nxt = jnp.where(n == last, bot_ref[:, s], p_next[:, s])
        q_ref[:, (l + 1) * cells:(l + 2) * cells] = left_sweep(prev, p_mid[:, s], nxt, wide)
    for l in range(lines):
        mid = q_ref[:, (l + 1) * cells:(l + 2) * cells]
        s = slice(l * cells, (l + 1) * cells)
        f_ref[:, s] = (centre_weight * mid + wr_ref[0:1, s] * q_ref[:, (l + 2) * cells:(l + 3) * cells]
                       + wr_ref[1:2, s] * q_ref[:, l * cells:(l + 1) * cells]
                       + wr_ref[2:3, s] * pltpu.roll(mid, cells - 1, 1) + wr_ref[3:4, s] * pltpu.roll(mid, 1, 1))

def forecast(wl, wr, top, p, bot, lo, hi, cells):
    rows, cols = p.shape
    steps = rows // cells
    whole = lambda x: pl.BlockSpec(x.shape, lambda n: (0, 0), pipeline_mode=pl.Buffered(1))
    blk = lambda f: pl.BlockSpec((cells, cols), f)
    return pl.pallas_call(f_kernel, grid=(steps,),
        out_shape=jax.ShapeDtypeStruct((rows, cols), F32),
        in_specs=[pl.BlockSpec((cells, 4), lambda n: (n, 0)), whole(wr), whole(top),
                  blk(lambda n: (jnp.maximum(n - 1, 0), 0)), blk(lambda n: (n, 0)),
                  blk(lambda n: (jnp.minimum(n + 1, steps - 1), 0)), whole(bot), whole(lo), whole(hi)],
        out_specs=blk(lambda n: (n, 0)),
        scratch_shapes=[pltpu.VMEM((cells, cols + 2 * cells), F32)],
        compiler_params=pltpu.CompilerParams(vmem_limit_bytes=40 << 20),
        cost_estimate=pl.CostEstimate(flops=5 * 10**7, bytes_accessed=32 << 20, transcendentals=0),
    )(wl, wr, top, p, p, p, bot, lo, hi)

def fin_kernel(f_ref, g_ref, s_ref, gc_ref, o_ref, wh, wlo):
    @pl.when(pl.program_id(0) == 0)
    def _():
        w = jnp.dot(g_ref[...], s_ref[...], precision=HI, preferred_element_type=F32)
        h, l = split(w)
        wh[...] = h
        wlo[...] = l
    o_ref[...] = f_ref[...] - dot3((wh[...], wlo[...]), split(gc_ref[...]), ((1,), (1,)))

def finish(f, g, s, gc, tile=256):
    rows, cols = f.shape
    count = s.shape[0]
    whole = lambda x: pl.BlockSpec(x.shape, lambda n: (0, 0), pipeline_mode=pl.Buffered(1))
    return pl.pallas_call(fin_kernel, grid=(cols // tile,),
        out_shape=jax.ShapeDtypeStruct((rows, cols), F32),
        in_specs=[pl.BlockSpec((rows, tile), lambda n: (0, n)), whole(g), whole(s), pl.BlockSpec((tile, count), lambda n: (n, 0))],
        out_specs=pl.BlockSpec((rows, tile), lambda n: (0, n)),
        scratch_shapes=[pltpu.VMEM((rows, count), BF16), pltpu.VMEM((rows, count), BF16)],
        compiler_params=pltpu.CompilerParams(vmem_limit_bytes=40 << 20),
        cost_estimate=pl.CostEstimate(flops=8 * 10**9, bytes_accessed=24 << 20, transcendentals=0),
    )(f, g, s, gc)


def pick_row(a, k):
    return jnp.broadcast_to(a[k:k + 1, :], a.shape)

def pick_col(a, k):
    return jnp.broadcast_to(a[:, k:k + 1], a.shape)

def invert_tile(a, pivots):
    n = a.shape[0]
    rid = lax.broadcasted_iota(jnp.int32, a.shape, 0)
    cid = lax.broadcasted_iota(jnp.int32, a.shape, 1)
    for k in range(0, n, pivots):
        if pivots == 1:
            row = a[k:k+1, :]
            col = pick_col(a, k)
            p = col[k:k+1, :]
            q = 1.0 / p
            r = row * q
            lane = cid[:1] == k
            r2 = jnp.where(lane, q, r)
            base = jnp.where(cid == k, 0.0, a)
            upd = base - col * r2
            a = jnp.where(rid == k, r2, upd)
        else:
            row0, row1 = a[k:k+1, :], a[k+1:k+2, :]
            col0, col1 = pick_col(a, k), pick_col(a, k + 1)
            p00, p10, p11 = col0[k:k+1, :], col0[k+1:k+2, :], col1[k+1:k+2, :]
            det = 1.0 / (p00 * p11 - p10 * p10)
            i00, i01, i11 = p11 * det, -p10 * det, p00 * det
            lane0, lane1 = cid[:1] == k, cid[:1] == k + 1
            r0 = jnp.where(lane0, i00, jnp.where(lane1, i01, i00 * row0 + i01 * row1))
            r1 = jnp.where(lane0, i01, jnp.where(lane1, i11, i01 * row0 + i11 * row1))
            base = jnp.where((cid == k) | (cid == k + 1), 0.0, a)
            upd = base - col0 * r0 - col1 * r1
            a = jnp.where(rid == k, r0, jnp.where(rid == k + 1, r1, upd))
    return a

def inv_kernel(s_ref, o_ref, *, pivots, block, prec=HI):
    n = s_ref.shape[0]
    s = s_ref[...]
    o_ref[...] = 0.5 * (s + s.T)
    nb = n // block

    def step(k, _):
        lo = pl.multiple_of(k * block, block)
        d = invert_tile(o_ref[pl.ds(lo, block), pl.ds(lo, block)], pivots)
        panel = o_ref[pl.ds(lo, block), :]
        col = o_ref[:, pl.ds(lo, block)]
        cid = lax.broadcasted_iota(jnp.int32, panel.shape, 1)
        dfull = jnp.concatenate([d] * nb, axis=1)
        inside = (cid >= lo) & (cid < lo + block)
        r = jnp.where(inside, dfull, jnp.dot(d, panel, precision=prec, preferred_element_type=jnp.float32))
        cid2 = lax.broadcasted_iota(jnp.int32, (n, n), 1)
        rest = jnp.where((cid2 >= lo) & (cid2 < lo + block), 0.0, o_ref[...])
        o_ref[...] = rest - jnp.dot(col, r, precision=prec, preferred_element_type=jnp.float32)
        o_ref[pl.ds(lo, block), :] = r
        return 0
    lax.fori_loop(0, nb, step, 0)

def invert(s, pivots=1, block=128):
    return pl.pallas_call(functools.partial(inv_kernel, pivots=pivots, block=block),
        out_shape=jax.ShapeDtypeStruct(s.shape, jnp.float32),
        in_specs=[pl.BlockSpec(memory_space=pltpu.VMEM)], out_specs=pl.BlockSpec(memory_space=pltpu.VMEM))(s)

def m_kernel(wl_ref, top_ref, t_ref, bot_ref, o_ref):
    cells, count = top_ref.shape
    lines = t_ref.shape[0] // cells
    for l in range(lines):
        s = slice(l * cells, (l + 1) * cells)
        wide = [jnp.broadcast_to(wl_ref[s, m:m + 1], (cells, count)) for m in range(4)]
        prev = top_ref[...] if l == 0 else t_ref[(l - 1) * cells:l * cells, :]
        nxt = bot_ref[...] if l == lines - 1 else t_ref[(l + 1) * cells:(l + 2) * cells, :]
        o_ref[s, :] = left_sweep(prev, t_ref[s, :], nxt, wide)


def sweep_panel(wl, top, t, bot):
    v = pl.BlockSpec(memory_space=pltpu.VMEM)
    return pl.pallas_call(m_kernel, out_shape=jax.ShapeDtypeStruct(t.shape, F32), in_specs=[v] * 4, out_specs=v,
        cost_estimate=pl.CostEstimate(flops=10**7, bytes_accessed=5 << 20, transcendentals=0))(wl, top, t, bot)


def sides(block, axis, dim, width):
    count = lax.axis_size(axis)
    forward = [(i, i + 1) for i in range(count - 1)]
    backward = [(target, source) for source, target in forward]
    low = lax.ppermute(lax.slice_in_dim(block, block.shape[dim] - width, None, axis=dim), axis, forward)
    high = lax.ppermute(lax.slice_in_dim(block, 0, width, axis=dim), axis, backward)
    return low, high


def cell_weights(vel_first, vel_second, start, lines):
    first = lax.dynamic_slice_in_dim(vel_first, start, lines, 0)
    second = lax.dynamic_slice_in_dim(vel_second, start, lines, 0)
    at = lax.broadcasted_iota(jnp.int32, second.shape, 1)
    ends = second.shape[1] - 1
    return [w.reshape(-1) for w in (
        dispersion - 0.5 * first,
        dispersion + 0.5 * first,
        jnp.where(at == ends, 0.0, dispersion - 0.5 * second),
        jnp.where(at == 0, 0.0, dispersion + 0.5 * second))]


def body(prior, vel_first, vel_second, obs_cell, obs_noise):
    rows, cols = prior.shape
    cells = vel_first.shape[0]
    row_lines, col_lines = rows // cells, cols // cells
    row_place, col_place = lax.axis_index("row"), lax.axis_index("col")
    row_count, col_count = lax.axis_size("row"), lax.axis_size("col")
    place = jnp.stack([row_place * row_lines, col_place * col_lines]).astype(jnp.int32)
    wl = jnp.stack(cell_weights(vel_first, vel_second, row_place * row_lines, row_lines), axis=1)
    wr = jnp.stack(cell_weights(vel_first, vel_second, col_place * col_lines, col_lines), axis=0)
    oi, oj = obs_cell[:, 0][None], obs_cell[:, 1][None]

    t_part, s_part = partials(place, prior, vel_first, vel_second, oi, oj)
    s_total = lax.psum(s_part, ("row", "col"))
    t_top, t_bot = sides(t_part, "row", 0, cells)
    g_part = sweep_panel(wl, t_top, t_part, t_bot)
    g_line = lax.psum_scatter(g_part, "col", scatter_dimension=0, tiled=True)
    blocks = cols // rows
    perm = []
    for r in range(row_count):
        for c in range(col_count):
            perm.append((r * col_count + c, ((r % blocks) * col_count + c) * col_count + r // blocks))
    g_rows = lax.all_gather(g_line, "col", axis=0, tiled=True)
    g_cols = lax.all_gather(lax.ppermute(g_line, ("row", "col"), perm), "row", axis=0, tiled=True)

    lo, hi = sides(prior, "col", 1, cells)
    top, bot = sides(prior, "row", 0, cells)
    lo_top, lo_bot = sides(lo, "row", 0, cells)
    hi_top, hi_bot = sides(hi, "row", 0, cells)
    lo = jnp.concatenate([lo_top, lo, lo_bot], axis=0)
    hi = jnp.concatenate([hi_top, hi, hi_bot], axis=0)
    field = forecast(wl, wr, top, prior, bot, lo, hi, cells)

    s_inv = invert(s_total + jnp.diag(obs_noise), 2, 128)
    return finish(field, g_rows, s_inv, g_cols, tile=512)


def solution(mesh):
    placed = (P("row", "col"), P(), P(), P(), P())
    return jax.shard_map(body, mesh=mesh, in_specs=placed, out_specs=P("row", "col"), check_vma=False)
```

time: 550 us -> 321 us (0.58)
  other arithmetic: 188 us -> 5.57 us
  local copies, waits for them, and re-layouts: 134 us -> 19.5 us
  Pallas kernels: 0 us -> 88.3 us
  matrix products: 39.4 us -> 0 us
  starting transfers between devices: 13.6 us -> 41.6 us
    another operation x18 -> x3, other arithmetic: 119 us -> 0.63 us  [the longest x1 0.58 us: body(): jnp.stack([row_place * row_lines, col_place * col_lines]).astype(jnp.int32)]
    pallas_call x0 -> x5, Pallas kernels: none -> 88.3 us  [the longest x1 39.5 us: invert(): pl.pallas_call(functools.partial(inv_kernel, pivots=pivots, block=block),...]
    psum x2 -> x1, waiting for transfers between devices: 142 us -> 95.2 us  [body(): s_total = lax.psum(s_part, ('row', 'col'))]
    gather x3 -> x0, local copies, waits for them, and re-layouts: 46.2 us -> none  [the longest x1 20.1 us: body(): jnp.take(prior_mean_vector, horizontal_slot, axis=0)]
    slice x7 -> x5, local copies, waits for them, and re-layouts: 53.2 us -> 7.35 us  [the longest x3 6.46 us: sides(): lax.slice_in_dim(block, 0, width, axis=dim)]
    reduce_scatter x0 -> x1, waiting for transfers between devices: none -> 37.5 us  [body(): g_line = lax.psum_scatter(g_part, 'col', scatter_dimension=0, tiled=True)]
    dot_general x3 -> x0, matrix products: 28.8 us -> none  [the longest x1 16.1 us: body(): jnp.dot(update_rows, update_cols, precision=finest_accuracy, preferred_el...]
    ppermute x4 -> x11, starting transfers between devices: 13.5 us -> 41.4 us  [the longest x5 27.7 us: sides(): lax.ppermute(lax.slice_in_dim(block, block.shape[dim] - width, None, axis...]
  transfers between devices with their start and end apart: 6 -> 15, of which waited for: 4 -> 6; matrix products, arithmetic and copies ran while one was open for 12% -> 4% of each run, Pallas kernels for 0% -> 17%
where the time goes in v1:
time: 321 us; the launch traced here: 316 us
  waiting for transfers between devices  146 us (45%)
  Pallas kernels  88.3 us (28%)
  starting transfers between devices  41.6 us (13%)
  local copies, waits for them, and re-layouts  19.5 us (6%)
  between operations  14.8 us (5%)
  other arithmetic  5.57 us (2%)
    psum x1, waiting for transfers between devices, body(): s_total = lax.psum(s_part, ('row', 'col'))  95.2 us
    pallas_call x1, Pallas kernels, invert(): pl.pallas_call(functools.partial(inv_kernel, pivots=pivots, block=block),...  39.5 us
    reduce_scatter x1, waiting for transfers between devices, body(): g_line = lax.psum_scatter(g_part, 'col', scatter_dimension=0, tiled=True)  37.5 us
    ppermute x5, starting transfers between devices, sides(): lax.ppermute(lax.slice_in_dim(block, block.shape[dim] - width, None, axis...  27.7 us
    pallas_call x1, Pallas kernels, partials(): pl.pallas_call(functools.partial(t_kernel, tile=tile), out_shape=(jax.Sha...  15.4 us
    pallas_call x1, Pallas kernels, forecast(): pl.pallas_call(f_kernel, grid=(steps,), out_shape=jax.ShapeDtypeStruct((r...  14.5 us
    pallas_call x1, Pallas kernels, finish(): pl.pallas_call(fin_kernel, grid=(cols // tile,), out_shape=jax.ShapeDtype...  14.3 us
    unnamed x18, local copies, waits for them, and re-layouts  9.7 us
  transfers between devices with their start and end apart: 15, of which 6 were waited for; matrix products, arithmetic and copies ran while one was open for 4% of the time, Pallas kernels for 17%

profile of v1, /device:TPU:1, one launch (start us, length us, event | category | flops | bytes accessed | tf_op | source)
XLA Modules:
  0.0 316.1 jit_solution(7557334454619256451)
XLA Ops:
  7.4 1.4 slice_bitcast_fusion
  9.3 15.4 %shard_map.56 = (f32[1024,512]{1,0:T(8,128)}, f32[512,512]{1,0:T(8,128)}) custom-call(s32[2]{0:T(128)} %pad_add_fusion.place_ref, f32[1024,2048]{1,0:T(8,128)} %p_hbm.1, f32[128,128]{1,0:T(8,128)} %velf_ref.1, f32[128,128]{1,0:T(8,128)} %vels_ref.1, s32[1,512]{1,0:T(1,128)} %get-tuple-element.28.oi_ref, s32[1,512]{1,0:T(1,128)} %get-tuple-element.27.oj_ref), custom_call_target="tpu_custom_call" | custom-call | flops 8000000000 | bytes 12582912 | tf_op jit(solution)/shard_map/pallas_call | solution.py:96
  24.7 1.1 fusion.6
  25.8 1.3 collective-permute-start.9
  27.1 5.0 %collective-permute-start.8 = (f32[128,512]{1,0:T(8,128)S(1)}, f32[128,512]{1,0:T(8,128)S(1)}, u32[]{:S(2)}, u32[]{:S(2)}) collective-permute-start(f32[128,512]{1,0:T(8,128)S(1)} %get-tuple-element.14), channel_id=1, source_target_pairs={{0,8},{8,16},{16,24},{24,32},{32,40},{40,48},{48,56},{56,64},{64,7... | collective-permute-start | bytes 786440 | tf_op jit(solution)/shard_map/ppermute | solution.py:261
  32.9 1.1 copy.10.wl_ref
  34.0 2.2 collective-permute-done.9.bot_ref
  37.8 4.5 %shard_map.57 = f32[1024,512]{1,0:T(8,128)} custom-call(f32[1024,4]{1,0:T(8,128)} %copy.10.wl_ref, f32[128,512]{1,0:T(8,128)} %copy-done.6, f32[1024,512]{1,0:T(8,128)} %get-tuple-element.7.t_ref, f32[128,512]{1,0:T(8,128)} %copy-done.5), custom_call_target="tpu_custom_call" | custom-call | flops 10000000 | bytes 5242880 | tf_op jit(solution)/shard_map/pallas_call | solution.py:253
  42.9 37.5 %reduce-scatter.2.cloned.1.call-done = f32[128,512]{1,0:T(8,128)} async-done(((f32[1024,512]{1,0:T(8,128)}), f32[128,512]{1,0:T(8,128)}) %reduce-scatter.2.cloned.1.call-update) | async-done | bytes 262160 | tf_op jit(solution)/shard_map/reduce_scatter | solution.py:293
  80.5 6.5 %collective-permute-start.10 = (f32[128,512]{1,0:T(8,128)}, f32[128,512]{1,0:T(8,128)S(1)}, u32[]{:S(2)}, u32[]{:S(2)}) collective-permute-start(f32[128,512]{1,0:T(8,128)} %reduce-scatter.2.cloned.1.call-done), channel_id=1, source_target_pairs={{0,0},{1,8},{2,16},{3,24},{4,32},{5,40},{6,48},{7,56},{8,64},{9,72... | collective-permute-start | bytes 786440 | tf_op jit(solution)/shard_map/ppermute | solution.py:300
  86.9 7.7 %collective-permute-done.10 = f32[128,512]{1,0:T(8,128)S(1)} collective-permute-done((f32[128,512]{1,0:T(8,128)}, f32[128,512]{1,0:T(8,128)S(1)}, u32[]{:S(2)}, u32[]{:S(2)}) %collective-permute-start.10) | collective-permute-done | bytes 262176 | tf_op jit(solution)/shard_map/ppermute | solution.py:300
  95.4 2.3 fusion.4
  97.6 1.9 collective-permute-start.5
  99.6 12.3 %collective-permute-start.2 = (f32[1024,128]{1,0:T(8,128)}, f32[1024,128]{1,0:T(8,128)S(1)}, u32[]{:S(2)}, u32[]{:S(2)}) collective-permute-start(f32[1024,128]{1,0:T(8,128)} %get-tuple-element.10), channel_id=1, source_target_pairs={{0,1},{1,2},{2,3},{3,4},{4,5},{5,6},{6,7},{8,9},{9,10},{10,11},{11... | collective-permute-start | bytes 1572872 | tf_op jit(solution)/shard_map/ppermute | solution.py:261
  111.9 3.1 fusion.5
  115.0 1.3 collective-permute-start.1
  116.3 4.1 %collective-permute-start = (f32[128,2048]{1,0:T(8,128)}, f32[128,2048]{1,0:T(8,128)S(1)}, u32[]{:S(2)}, u32[]{:S(2)}) collective-permute-start(f32[128,2048]{1,0:T(8,128)} %get-tuple-element.12), channel_id=1, source_target_pairs={{0,8},{8,16},{16,24},{24,32},{32,40},{40,48},{48,56},{56,64},{64,7... | collective-permute-start | bytes 3145736 | tf_op jit(solution)/shard_map/ppermute | solution.py:261
  121.1 95.2 %all-reduce.2.cloned.1.call-done = f32[512,512]{1,0:T(8,128)} async-done(((f32[512,512]{1,0:T(8,128)}), f32[512,512]{1,0:T(8,128)}) %all-reduce.2.cloned.1.call-update) | async-done | bytes 1048592 | tf_op jit(solution)/shard_map/psum | solution.py:290
  216.3 2.3 select_add_fusion.s_ref
  218.7 39.5 %shard_map.58.s_ref = f32[512,512]{1,0:T(8,128)} custom-call(f32[512,512]{1,0:T(8,128)} %select_add_fusion.s_ref), custom_call_target="tpu_custom_call" | custom-call | tf_op jit(solution)/shard_map/pallas_call | solution.py:236
  259.1 2.3 collective-permute-start.6
  261.4 1.3 collective-permute-start.7
  262.7 4.0 %collective-permute-start.3 = (f32[128,128]{1,0:T(8,128)S(1)}, f32[128,128]{1,0:T(8,128)S(1)}, u32[]{:S(2)}, u32[]{:S(2)}) collective-permute-start(f32[128,128]{1,0:T(8,128)S(1)} %get-tuple-element.17), channel_id=1, source_target_pairs={{0,8},{8,16},{16,24},{24,32},{32,40},{40,48},{48,56},{56,64},{64,7... | collective-permute-start | bytes 196616 | tf_op jit(solution)/shard_map/ppermute | solution.py:261
  266.8 1.5 collective-permute-start.4
  268.2 1.1 pad_maximum_fusion.1.hi_ref
  269.3 2.4 collective-permute-done.4
  271.8 14.5 %shard_map.55.f_ref = f32[1024,2048]{1,0:T(8,128)S(1)} custom-call(f32[1024,4]{1,0:T(8,128)S(1)} %copy-done.1, f32[4,2048]{1,0:T(4,128)S(1)} %pad_maximum_fusion.2.wr_ref, f32[128,2048]{1,0:T(8,128)S(1)} %collective-permute-done.top_ref, f32[1024,2048]{1,0:T(8,128)} %p_hbm.1, f32[1024,2048]{1,0:T(8,128)} %p_hbm.1, f32[1024,2048]{1,0:T(8,128)} %p_hbm.1, ...), custom_call_target="tpu_custom_call" | custom-call | flops 50000000 | bytes 33554432 | tf_op jit(solution)/shard_map/pallas_call | solution.py:143
  286.4 3.3 %copy-done = f32[1024,2048]{1,0:T(8,128)} copy-done((f32[1024,2048]{1,0:T(8,128)}, f32[1024,2048]{1,0:T(8,128)S(1)}, u32[]{:S(2)}) %copy-start) | copy-done | bytes 8388632
  289.6 1.2 copy-done.2
  290.9 2.2 copy-done.3
  293.1 1.6 copy-done.4
  294.6 14.3 %shard_map.59 = f32[1024,2048]{1,0:T(8,128)} custom-call(f32[1024,2048]{1,0:T(8,128)} %copy-done, f32[1024,512]{1,0:T(8,128)S(1)} %copy-done.4, f32[512,512]{1,0:T(8,128)S(1)} %copy-done.2, f32[2048,512]{1,0:T(8,128)S(1)} %copy-done.3), custom_call_target="tpu_custom_call" | custom-call | flops 8000000000 | bytes 25165824 | tf_op jit(solution)/shard_map/pallas_call | solution.py:167
  (42 shorter events, 6.1 us)
Async XLA Ops:
  7.4 73.0 %reduce-scatter.2.cloned.1.call-start = ((), (), s32[]{:S(2)}) async-start(), calls=%async_computation.1 | async-start | bytes 2359296 | tf_op jit(solution)/shard_map/reduce_scatter | solution.py:293
  24.7 191.6 %copy-start.8 = (f32[512]{0:T(512)S(1)}, f32[512]{0:T(512)}, u32[]{:S(2)}) copy-start(f32[512]{0:T(512)} %param.9) | copy-start | bytes 6148
  25.8 10.4 %collective-permute-start.9 = (f32[128,512]{1,0:T(8,128)S(1)}, f32[128,512]{1,0:T(8,128)S(1)}, u32[]{:S(2)}, u32[]{:S(2)}) collective-permute-start(f32[128,512]{1,0:T(8,128)S(1)} %get-tuple-element.13), channel_id=1, source_target_pairs={{8,0},{16,8},{24,16},{32,24},{40,32},{48,40},{56,48},{64,56},{72,6... | collective-permute-start | bytes 786440 | tf_op jit(solution)/shard_map/ppermute | solution.py:262
  27.1 10.0 %collective-permute-start.8 = (f32[128,512]{1,0:T(8,128)S(1)}, f32[128,512]{1,0:T(8,128)S(1)}, u32[]{:S(2)}, u32[]{:S(2)}) collective-permute-start(f32[128,512]{1,0:T(8,128)S(1)} %get-tuple-element.14), channel_id=1, source_target_pairs={{0,8},{8,16},{16,24},{24,32},{32,40},{40,48},{48,56},{56,64},{64,7... | collective-permute-start | bytes 786440 | tf_op jit(solution)/shard_map/ppermute | solution.py:261
  36.2 0.9 copy-start.5
  37.1 0.7 copy-start.6
  42.2 229.6 %copy-start.1 = (f32[1024,4]{1,0:T(8,128)S(1)}, f32[1024,4]{1,0:T(8,128)}, u32[]{:S(2)}) copy-start(f32[1024,4]{1,0:T(8,128)} %copy.10.wl_ref) | copy-start | bytes 49156
  42.3 174.0 %all-reduce.2.cloned.1.call-start = ((), (), s32[]{:S(2)}) async-start(), calls=%async_computation.3 | async-start | bytes 2097152 | tf_op jit(solution)/shard_map/psum | solution.py:290
  42.9 246.8 %all-gather.3.cloned.1.call-start = ((), (), s32[]{:S(2)}) async-start(), calls=%async_computation.2 | async-start | bytes 2359296 | tf_op jit(solution)/shard_map/all_gather | solution.py:299
  80.4 209.2 %all-gather.5.cloned.1.call-start = ((), (), s32[]{:S(2)}) async-start(), calls=%async_computation.4 | async-start | bytes 4456448 | tf_op jit(solution)/shard_map/all_gather | solution.py:300
  80.5 14.2 %collective-permute-start.10 = (f32[128,512]{1,0:T(8,128)}, f32[128,512]{1,0:T(8,128)S(1)}, u32[]{:S(2)}, u32[]{:S(2)}) collective-permute-start(f32[128,512]{1,0:T(8,128)} %reduce-scatter.2.cloned.1.call-done), channel_id=1, source_target_pairs={{0,0},{1,8},{2,16},{3,24},{4,32},{5,40},{6,48},{7,56},{8,64},{9,72... | collective-permute-start | bytes 786440 | tf_op jit(solution)/shard_map/ppermute | solution.py:300
  94.6 0.7 copy-start.7
  97.6 160.6 %collective-permute-start.5 = (f32[1024,128]{1,0:T(8,128)}, f32[1024,128]{1,0:T(8,128)}, u32[]{:S(2)}, u32[]{:S(2)}) collective-permute-start(f32[1024,128]{1,0:T(8,128)} %get-tuple-element.9), channel_id=1, source_target_pairs={{1,0},{2,1},{3,2},{4,3},{5,4},{6,5},{7,6},{9,8},{10,9},{11,10},{12... | collective-permute-start | bytes 1572872 | tf_op jit(solution)/shard_map/ppermute | solution.py:262
  99.6 163.2 %collective-permute-start.2 = (f32[1024,128]{1,0:T(8,128)}, f32[1024,128]{1,0:T(8,128)S(1)}, u32[]{:S(2)}, u32[]{:S(2)}) collective-permute-start(f32[1024,128]{1,0:T(8,128)} %get-tuple-element.10), channel_id=1, source_target_pairs={{0,1},{1,2},{2,3},{3,4},{4,5},{5,6},{6,7},{8,9},{9,10},{10,11},{11... | collective-permute-start | bytes 1572872 | tf_op jit(solution)/shard_map/ppermute | solution.py:261
  115.0 156.8 %collective-permute-start.1 = (f32[128,2048]{1,0:T(8,128)}, f32[128,2048]{1,0:T(8,128)S(1)}, u32[]{:S(2)}, u32[]{:S(2)}) collective-permute-start(f32[128,2048]{1,0:T(8,128)} %get-tuple-element.11), channel_id=1, source_target_pairs={{8,0},{16,8},{24,16},{32,24},{40,32},{48,40},{56,48},{64,56},{72,6... | collective-permute-start | bytes 3145736 | tf_op jit(solution)/shard_map/ppermute | solution.py:262
  116.3 155.5 %collective-permute-start = (f32[128,2048]{1,0:T(8,128)}, f32[128,2048]{1,0:T(8,128)S(1)}, u32[]{:S(2)}, u32[]{:S(2)}) collective-permute-start(f32[128,2048]{1,0:T(8,128)} %get-tuple-element.12), channel_id=1, source_target_pairs={{0,8},{8,16},{16,24},{24,32},{32,40},{40,48},{48,56},{56,64},{64,7... | collective-permute-start | bytes 3145736 | tf_op jit(solution)/shard_map/ppermute | solution.py:261
  259.1 7.7 %collective-permute-start.6 = (f32[128,128]{1,0:T(8,128)S(1)}, f32[128,128]{1,0:T(8,128)S(1)}, u32[]{:S(2)}, u32[]{:S(2)}) collective-permute-start(f32[128,128]{1,0:T(8,128)S(1)} %get-tuple-element.15), channel_id=1, source_target_pairs={{0,8},{8,16},{16,24},{24,32},{32,40},{40,48},{48,56},{56,64},{64,7... | collective-permute-start | bytes 196616 | tf_op jit(solution)/shard_map/ppermute | solution.py:261
  261.4 6.8 %collective-permute-start.7 = (f32[128,128]{1,0:T(8,128)S(1)}, f32[128,128]{1,0:T(8,128)S(1)}, u32[]{:S(2)}, u32[]{:S(2)}) collective-permute-start(f32[128,128]{1,0:T(8,128)S(1)} %get-tuple-element.16), channel_id=1, source_target_pairs={{8,0},{16,8},{24,16},{32,24},{40,32},{48,40},{56,48},{64,56},{72,6... | collective-permute-start | bytes 196616 | tf_op jit(solution)/shard_map/ppermute | solution.py:262
  262.7 6.6 %collective-permute-start.3 = (f32[128,128]{1,0:T(8,128)S(1)}, f32[128,128]{1,0:T(8,128)S(1)}, u32[]{:S(2)}, u32[]{:S(2)}) collective-permute-start(f32[128,128]{1,0:T(8,128)S(1)} %get-tuple-element.17), channel_id=1, source_target_pairs={{0,8},{8,16},{16,24},{24,32},{32,40},{40,48},{48,56},{56,64},{64,7... | collective-permute-start | bytes 196616 | tf_op jit(solution)/shard_map/ppermute | solution.py:261
  266.8 5.0 %collective-permute-start.4 = (f32[128,128]{1,0:T(8,128)S(1)}, f32[128,128]{1,0:T(8,128)S(1)}, u32[]{:S(2)}, u32[]{:S(2)}) collective-permute-start(f32[128,128]{1,0:T(8,128)S(1)} %get-tuple-element.18), channel_id=1, source_target_pairs={{8,0},{16,8},{24,16},{32,24},{40,32},{48,40},{56,48},{64,56},{72,6... | collective-permute-start | bytes 196616 | tf_op jit(solution)/shard_map/ppermute | solution.py:262
  286.4 3.3 %copy-start = (f32[1024,2048]{1,0:T(8,128)}, f32[1024,2048]{1,0:T(8,128)S(1)}, u32[]{:S(2)}) copy-start(f32[1024,2048]{1,0:T(8,128)S(1)} %shard_map.55.f_ref) | copy-start | bytes 25165828
  289.6 1.2 copy-start.2
  290.9 2.2 copy-start.3
  293.1 1.6 copy-start.4
Sparse Core Ops, SparseCore 0:
  42.4 37.9 reduce-scatter.1
  82.1 32.0 all-gather.2
  116.3 60.3 all-gather.4
Sparse Core Ops, SparseCore 1:
  47.5 168.7 all-reduce.1

commit v2 on v1

--- a/solution.py
+++ b/solution.py
@@ -54,8 +54,9 @@
         out = jnp.where(jid == oj + dj, row, out)
     return out
 
-def t_kernel(place_ref, p_hbm, velf_ref, vels_ref, oi_ref, oj_ref, t_ref, s_ref, buf, ch, cl, wsc, sems, *, tile):
+def observed_panel(first_row, first_col, p_hbm, velf_ref, vels_ref, oi_ref, oj_ref, t_ref, s_ref, buf, ch, cl, wsc, sems):
     rows, cols = p_hbm.shape
+    tile = buf.shape[1]
     cells = velf_ref.shape[0]
     steps = rows // tile
     def fetch(n):
@@ -64,7 +65,6 @@
         fetch(n).start()
     oi, oj = oi_ref[...], oj_ref[...]
     w = observed_weights(velf_ref, vels_ref, oi, oj)
-    first_row, first_col = place_ref[0], place_ref[1]
     keys = sorted(w)
     for n, key in enumerate(keys):
         wsc[n:n + 1, :] = w[key]
@@ -89,21 +89,6 @@
         return 0
     lax.fori_loop(0, steps, run, 0)
 
-def partials(place, p, velf, vels, oi, oj, tile=256):
-    rows, cols = p.shape
-    count = oi.shape[1]
-    v = pl.BlockSpec(memory_space=pltpu.VMEM)
-    return pl.pallas_call(functools.partial(t_kernel, tile=tile),
-        out_shape=(jax.ShapeDtypeStruct((rows, count), F32), jax.ShapeDtypeStruct((count, count), F32)),
-        in_specs=[pl.BlockSpec(memory_space=pltpu.SMEM), pl.BlockSpec(memory_space=pl.ANY), v, v, v, v],
-        out_specs=(v, v),
-        scratch_shapes=[pltpu.VMEM((rows // tile, tile, cols), F32), pltpu.VMEM((cols, count), BF16),
-                        pltpu.VMEM((cols, count), BF16), pltpu.VMEM((16, count), F32),
-                        pltpu.SemaphoreType.DMA((rows // tile,))],
-        compiler_params=pltpu.CompilerParams(vmem_limit_bytes=60 << 20),
-        cost_estimate=pl.CostEstimate(flops=8 * 10**9, bytes_accessed=12 << 20, transcendentals=0),
-    )(place, p, velf, vels, oi, oj)
-
 
 def left_sweep(prev, mid, nxt, w):
     cells = mid.shape[0]
@@ -174,103 +159,399 @@
     )(f, g, s, gc)
 
 
-def pick_row(a, k):
-    return jnp.broadcast_to(a[k:k + 1, :], a.shape)
-
-def pick_col(a, k):
-    return jnp.broadcast_to(a[:, k:k + 1], a.shape)
-
-def invert_tile(a, pivots):
-    n = a.shape[0]
+def invert_in(s_ref, noise_ref, o_ref, hooks, block=128):
+    n = s_ref.shape[0]
+    s = s_ref[...]
+    rid = lax.broadcasted_iota(jnp.int32, (n, n), 0)
+    cid = lax.broadcasted_iota(jnp.int32, (n, n), 1)
+    o_ref[...] = 0.5 * (s + s.T) + jnp.where(rid == cid, noise_ref[...], 0.0)
+    nb = n // block
+    for k in range(nb):
+        lo = k * block
+        own = slice(lo, lo + block)
+        a = o_ref[own, own]
+        for part in (0, 1):
+            if (k, part) in hooks:
+                hooks[k, part]()
+            a = pivot(a, range(part * block // 2, (part + 1) * block // 2, 2))
+        panel = jnp.dot(a, o_ref[own, :], precision=HI, preferred_element_type=F32)
+        col = o_ref[:, own]
+        for j in range(nb):
+            here = slice(j * block, (j + 1) * block)
+            r = a if j == k else panel[:, here]
+            upd = jnp.dot(col, r, precision=HI, preferred_element_type=F32)
+            o_ref[:, here] = -upd if j == k else o_ref[:, here] - upd
+            o_ref[own, here] = r
+
+
+def pivot(a, steps):
     rid = lax.broadcasted_iota(jnp.int32, a.shape, 0)
     cid = lax.broadcasted_iota(jnp.int32, a.shape, 1)
-    for k in range(0, n, pivots):
-        if pivots == 1:
-            row = a[k:k+1, :]
-            col = pick_col(a, k)
-            p = col[k:k+1, :]
-            q = 1.0 / p
-            r = row * q
-            lane = cid[:1] == k
-            r2 = jnp.where(lane, q, r)
-            base = jnp.where(cid == k, 0.0, a)
-            upd = base - col * r2
-            a = jnp.where(rid == k, r2, upd)
-        else:
-            row0, row1 = a[k:k+1, :], a[k+1:k+2, :]
-            col0, col1 = pick_col(a, k), pick_col(a, k + 1)
-            p00, p10, p11 = col0[k:k+1, :], col0[k+1:k+2, :], col1[k+1:k+2, :]
-            det = 1.0 / (p00 * p11 - p10 * p10)
-            i00, i01, i11 = p11 * det, -p10 * det, p00 * det
-            lane0, lane1 = cid[:1] == k, cid[:1] == k + 1
-            r0 = jnp.where(lane0, i00, jnp.where(lane1, i01, i00 * row0 + i01 * row1))
-            r1 = jnp.where(lane0, i01, jnp.where(lane1, i11, i01 * row0 + i11 * row1))
-            base = jnp.where((cid == k) | (cid == k + 1), 0.0, a)
-            upd = base - col0 * r0 - col1 * r1
-            a = jnp.where(rid == k, r0, jnp.where(rid == k + 1, r1, upd))
+    for k in steps:
+        row0, row1 = a[k:k + 1, :], a[k + 1:k + 2, :]
+        col0 = jnp.broadcast_to(a[:, k:k + 1], a.shape)
+        col1 = jnp.broadcast_to(a[:, k + 1:k + 2], a.shape)
+        p00, p10, p11 = col0[k:k + 1, :], col0[k + 1:k + 2, :], col1[k + 1:k + 2, :]
+        det = 1.0 / (p00 * p11 - p10 * p10)
+        i00, i01, i11 = p11 * det, -p10 * det, p00 * det
+        lane0, lane1 = cid[:1] == k, cid[:1] == k + 1
+        r0 = jnp.where(lane0, i00, jnp.where(lane1, i01, i00 * row0 + i01 * row1))
+        r1 = jnp.where(lane0, i01, jnp.where(lane1, i11, i01 * row0 + i11 * row1))
+        base = jnp.where((cid == k) | (cid == k + 1), 0.0, a)
+        upd = base - col0 * r0 - col1 * r1
+        a = jnp.where(rid == k, r0, jnp.where(rid == k + 1, r1, upd))
     return a
 
-def inv_kernel(s_ref, o_ref, *, pivots, block, prec=HI):
-    n = s_ref.shape[0]
-    s = s_ref[...]
-    o_ref[...] = 0.5 * (s + s.T)
-    nb = n // block
-
-    def step(k, _):
-        lo = pl.multiple_of(k * block, block)
-        d = invert_tile(o_ref[pl.ds(lo, block), pl.ds(lo, block)], pivots)
-        panel = o_ref[pl.ds(lo, block), :]
-        col = o_ref[:, pl.ds(lo, block)]
-        cid = lax.broadcasted_iota(jnp.int32, panel.shape, 1)
-        dfull = jnp.concatenate([d] * nb, axis=1)
-        inside = (cid >= lo) & (cid < lo + block)
-        r = jnp.where(inside, dfull, jnp.dot(d, panel, precision=prec, preferred_element_type=jnp.float32))
-        cid2 = lax.broadcasted_iota(jnp.int32, (n, n), 1)
-        rest = jnp.where((cid2 >= lo) & (cid2 < lo + block), 0.0, o_ref[...])
-        o_ref[...] = rest - jnp.dot(col, r, precision=prec, preferred_element_type=jnp.float32)
-        o_ref[pl.ds(lo, block), :] = r
-        return 0
-    lax.fori_loop(0, nb, step, 0)
-
-def invert(s, pivots=1, block=128):
-    return pl.pallas_call(functools.partial(inv_kernel, pivots=pivots, block=block),
-        out_shape=jax.ShapeDtypeStruct(s.shape, jnp.float32),
-        in_specs=[pl.BlockSpec(memory_space=pltpu.VMEM)], out_specs=pl.BlockSpec(memory_space=pltpu.VMEM))(s)
-
-def m_kernel(wl_ref, top_ref, t_ref, bot_ref, o_ref):
-    cells, count = top_ref.shape
-    lines = t_ref.shape[0] // cells
+
+MESH = pl.DeviceIdType.MESH
+RING = 4
+
+
+def exchange_kernel(p_hbm, velf_ref, vels_ref, oi_ref, oj_ref, noise_ref, wl_ref,
+                    sinv_ref, grow_ref, gcol_ref, top_ref, bot_ref, lo_ref, hi_ref,
+                    buf, ch, cl, wsc, t_ref, s_ref, th, gp, rg, gs, ry, rl,
+                    s_acc, r0, r1, r2, r3, s_out, in_sems, send_sems, recv_sems):
+    rows, cols = p_hbm.shape
+    cells, count = th.shape[1], th.shape[2]
+    row, col = lax.axis_index("row"), lax.axis_index("col")
+    row_count, col_count = lax.axis_size("row"), lax.axis_size("col")
+    x, z = row // RING, row % RING
+    y, core = col // 2, col % 2
+
+    def step(v, d):
+        return (v + d + RING) % RING
+
+    def chip(dx=0, dy=0, dz=0):
+        return (step(x, dx) * RING + step(z, dz), step(y, dy) * 2 + core)
+
+    partner = (row, col + 1 - 2 * core)
+    twin_row = y * RING + 2 * core + z % 2
+    twin_col = 2 * x + z // 2
+    twin = (twin_row, twin_col)
+    alone = (twin_row == row) & (twin_col == col)
+    up, down = (row + 1) % row_count, (row + row_count - 1) % row_count
+    right, left = (col + 1) % col_count, (col + col_count - 1) % col_count
+
+    barrier = pltpu.get_barrier_semaphore()
+    greeted = [partner, (up, col), (down, col), (row, right), (row, left),
+               (up, right), (up, left), (down, right), (down, left)]
+    greeted += [chip(dx=d) for d in (1, 2, 3)] + [chip(dy=d) for d in (1, 2, 3)] + [chip(dz=d) for d in (1, 2, 3)]
+    for peer in greeted:
+        pl.semaphore_signal(barrier, inc=1, device_id=peer, device_id_type=MESH)
+
+    @pl.when(jnp.logical_not(alone))
+    def _():
+        pl.semaphore_signal(barrier, inc=1, device_id=twin, device_id_type=MESH)
+    pl.semaphore_wait(barrier, len(greeted) + 1 - alone.astype(jnp.int32))
+
+    used, sent = {}, []
+
+    def slot(key):
+        if key not in used:
+            used[key] = len(used)
+        return used[key]
+
+    def copy(key, src, dst, peer):
+        n = slot(key)
+        return pltpu.make_async_remote_copy(src_ref=src, dst_ref=dst, send_sem=send_sems.at[n], recv_sem=recv_sems.at[n],
+                                            device_id=peer, device_id_type=MESH)
+
+    def send(key, src, dst, peer):
+        c = copy(key, src, dst, peer)
+        c.start()
+        sent.append(c)
+
+    def arrive(key, dst, peer):
+        copy(key, dst, dst, peer).wait_recv()
+
+    mid = pl.ds(cells, rows)
+    halo = [
+        ("p_up", p_hbm.at[pl.ds(rows - cells, cells), :], top_ref.at[:, :], (up, col), (down, col)),
+        ("p_down", p_hbm.at[pl.ds(0, cells), :], bot_ref.at[:, :], (down, col), (up, col)),
+        ("p_right", p_hbm.at[:, pl.ds(cols - cells, cells)], lo_ref.at[mid, :], (row, right), (row, left)),
+        ("p_left", p_hbm.at[:, pl.ds(0, cells)], hi_ref.at[mid, :], (row, left), (row, right)),
+        ("p_up_right", p_hbm.at[pl.ds(rows - cells, cells), pl.ds(cols - cells, cells)], lo_ref.at[pl.ds(0, cells), :],
+         (up, right), (down, left)),
+        ("p_up_left", p_hbm.at[pl.ds(rows - cells, cells), pl.ds(0, cells)], hi_ref.at[pl.ds(0, cells), :],
+         (up, left), (down, right)),
+        ("p_down_right", p_hbm.at[pl.ds(0, cells), pl.ds(cols - cells, cells)], lo_ref.at[pl.ds(rows + cells, cells), :],
+         (down, right), (up, left)),
+        ("p_down_left", p_hbm.at[pl.ds(0, cells), pl.ds(0, cells)], hi_ref.at[pl.ds(rows + cells, cells), :],
+         (down, left), (up, right)),
+    ]
+    for key, src, dst, to, _ in halo:
+        send(key, src, dst, to)
+
+    observed_panel(row * (rows // cells), col * (cols // cells), p_hbm, velf_ref, vels_ref, oi_ref, oj_ref, t_ref, s_ref,
+                   buf, ch, cl, wsc, in_sems)
+
+    send("t_up", t_ref.at[pl.ds(rows - cells, cells), :], th.at[0], (up, col))
+    send("t_down", t_ref.at[pl.ds(0, cells), :], th.at[1], (down, col))
+    half = count // 2
+    mine = pl.multiple_of(core * half, half)
+    other = pl.multiple_of(half - core * half, half)
+    send("s_core", s_ref.at[pl.ds(other, half), :], r0.at[:, :], partner)
+    arrive("s_core", r0.at[:, :], partner)
+    s_acc[pl.ds(mine, half), :] = s_ref[pl.ds(mine, half), :] + r0[...]
+
+    wide = count // 2
+    p1, p2, p3 = half // RING, half // RING**2, 8
+    order = (("x", "z"), ("z", "x"))
+    pos = {"x": x, "y": y, "z": z}
+
+    def at1(a, i):
+        return (pl.ds(pl.multiple_of(mine + i * p1, 8), p1), pl.ds(a * wide, wide))
+
+    def at2(a, i, j):
+        return (pl.ds(pl.multiple_of(mine + i * p1 + j * p2, 8), p2), pl.ds(a * wide, wide))
+
+    def at3(a, i, j, q):
+        return (pl.ds(pl.multiple_of(mine + i * p1 + j * p2 + (q // 2) * p3, 8), p3),
+                pl.ds(pl.multiple_of(a * wide + (q % 2) * 128, 128), 128))
+
+    def hop(axis, d):
+        return chip(**{"d" + axis: d})
+
+    def reduce_start(name, slots, place, axes):
+        for a in (0, 1):
+            for d in (1, 2, 3):
+                axis = axes[a]
+                send((name, a, d), s_acc.at[place(a, step(pos[axis], d))], slots.at[a, d - 1], hop(axis, d))
+
+    def reduce_end(name, slots, place, axes):
+        for a in (0, 1):
+            for d in (1, 2, 3):
+                arrive((name, a, d), slots.at[a, d - 1], hop(axes[a], -d))
+            here = place(a, pos[axes[a]])
+            s_acc[here] = (s_acc[here] + slots[a, 0]) + (slots[a, 1] + slots[a, 2])
+
+    def gather_start(name, place, axes):
+        for a in (0, 1):
+            here = place(a, pos[axes[a]])
+            for d in (1, 2, 3):
+                send((name, a, d), s_out.at[here], s_out.at[here], hop(axes[a], d))
+
+    def gather_end(name, place, axes):
+        for a in (0, 1):
+            for d in (1, 2, 3):
+                there = place(a, step(pos[axes[a]], -d))
+                arrive((name, a, d), s_out.at[there], hop(axes[a], -d))
+
+    axes1, axes2, axes3 = [o[0] for o in order], [o[1] for o in order], ["y", "y"]
+    own1 = [pos[a] for a in axes1]
+    own2 = [pos[a] for a in axes2]
+    place1 = at1
+    place2 = lambda a, j: at2(a, own1[a], j)
+    place3 = lambda a, q: at3(a, own1[a], own2[a], q)
+
+    reduce_start("s1", r1, place1, axes1)
+
+    arrive("t_up", th.at[0], (down, col))
+    arrive("t_down", th.at[1], (up, col))
+    lines = rows // cells
     for l in range(lines):
         s = slice(l * cells, (l + 1) * cells)
-        wide = [jnp.broadcast_to(wl_ref[s, m:m + 1], (cells, count)) for m in range(4)]
-        prev = top_ref[...] if l == 0 else t_ref[(l - 1) * cells:l * cells, :]
-        nxt = bot_ref[...] if l == lines - 1 else t_ref[(l + 1) * cells:(l + 2) * cells, :]
-        o_ref[s, :] = left_sweep(prev, t_ref[s, :], nxt, wide)
-
-
-def sweep_panel(wl, top, t, bot):
+        w = [jnp.broadcast_to(wl_ref[s, m:m + 1], (cells, count)) for m in range(4)]
+        prev = th[0] if l == 0 else t_ref[(l - 1) * cells:l * cells, :]
+        nxt = th[1] if l == lines - 1 else t_ref[(l + 1) * cells:(l + 2) * cells, :]
+        gp[l] = left_sweep(prev, t_ref[s, :], nxt, w)
+    for q in range(RING):
+        send(("g_core", q), gp.at[2 * q + 1 - core], rg.at[q], partner)
+
+    reduce_end("s1", r1, place1, axes1)
+    reduce_start("s2", r2, place2, axes2)
+
+    for q in range(RING):
+        arrive(("g_core", q), rg.at[q], partner)
+        gs[q] = gp[2 * q + core] + rg[q]
+    h = cells // 2
+    first, second = pl.ds(0, h), pl.ds(h, h)
+    far, nxt_y, prv_y = step(y, 2), step(y, 1), step(y, -1)
+    send("g_far_up", gs.at[far, first], ry.at[0], chip(dy=1))
+    send("g_far_down", gs.at[far, second], ry.at[1], chip(dy=-1))
+
+    reduce_end("s2", r2, place2, axes2)
+    reduce_start("s3", r3, place3, axes3)
+
+    arrive("g_far_up", ry.at[0], chip(dy=-1))
+    arrive("g_far_down", ry.at[1], chip(dy=1))
+    gs[nxt_y, first] = gs[nxt_y, first] + ry[0]
+    gs[prv_y, second] = gs[prv_y, second] + ry[1]
+    send("g_up", gs.at[nxt_y], rl.at[0], chip(dy=1))
+    send("g_down", gs.at[prv_y], rl.at[1], chip(dy=-1))
+
+    for a in (0, 1):
+        for d in (1, 2, 3):
+            arrive(("s3", a, d), r3.at[a, d - 1], hop("y", -d))
+        here = place3(a, y)
+        s_out[here] = (s_acc[here] + r3[a, 0]) + (r3[a, 1] + r3[a, 2])
+    gather_start("a3", place3, axes3)
+    gather_end("a3", place3, axes3)
+    gather_start("a2", place2, axes2)
+
+    arrive("g_up", rl.at[0], chip(dy=-1))
+    arrive("g_down", rl.at[1], chip(dy=1))
+
+    def line_at(c, lo=0, n=cells):
+        return (pl.ds(pl.multiple_of(c * cells + lo, 8), n), slice(None))
+
+    own = line_at(col)
+    grow_ref[own] = (gs[y] + rl[0]) + rl[1]
+
+    def col_line(xx, zz, lo=0, n=cells):
+        return line_at(8 * (zz % 2) + 2 * xx + zz // 2, lo, n)
+
+    landing = col_line(x, z)
+    away = line_at(8 * (row % 2) + col)
+    twin_copy = copy("twin", grow_ref.at[own], gcol_ref.at[away], twin)
+
+    @pl.when(alone)
+    def _():
+        gcol_ref[landing] = grow_ref[own]
+
+    @pl.when(jnp.logical_not(alone))
+    def _():
+        twin_copy.start()
+
+    send("y_up", grow_ref.at[own], grow_ref.at[own], chip(dy=1))
+    send("y_down", grow_ref.at[own], grow_ref.at[own], chip(dy=-1))
+    send(("c", 0), grow_ref.at[own], grow_ref.at[own], partner)
+
+    gather_end("a2", place2, axes2)
+    gather_start("a1", place1, axes1)
+    gather_end("a1", place1, axes1)
+    whole = (pl.ds(mine, half), slice(None))
+    send("s_back", s_out.at[whole], s_out.at[whole], partner)
+
+    def c_of(d):
+        return 2 * step(y, d) + core
+
+    def twin_landed():
+        @pl.when(jnp.logical_not(alone))
+        def _():
+            arrive("twin", gcol_ref.at[landing], twin)
+
+    lows = (0, h)
+    rings = (("x", "z"), ("z", "x"))
+
+    def piece(a, d0, d1, lo=0, n=h):
+        dx, dz = (d0, d1) if a == 0 else (d1, d0)
+        return gcol_ref.at[col_line(step(x, dx), step(z, dz), lows[a] + lo, n)]
+
+    def turn(a, level, d):
+        return hop(rings[a][level], d)
+
+    def p1():
+        twin_landed()
+        for a in (0, 1):
+            for d in (1, -1):
+                send(("q1", a, d), piece(a, 0, 0), piece(a, 0, 0), turn(a, 0, d))
+        for a in (0, 1):
+            for d in (1, -1):
+                send(("q2", a, 0, d), piece(a, 0, 0), piece(a, 0, 0), turn(a, 1, d))
+        arrive("y_up", grow_ref.at[line_at(c_of(-1))], chip(dy=-1))
+        arrive("y_down", grow_ref.at[line_at(c_of(1))], chip(dy=1))
+        send("y_far_up", grow_ref.at[line_at(c_of(-1), 0, h)], grow_ref.at[line_at(c_of(-1), 0, h)], chip(dy=1))
+        send("y_far_down", grow_ref.at[line_at(c_of(1), h, h)], grow_ref.at[line_at(c_of(1), h, h)], chip(dy=-1))
+        for d in (-1, 1):
+            send(("c", d), grow_ref.at[line_at(c_of(d))], grow_ref.at[line_at(c_of(d))], partner)
+
+    def p2():
+        for a in (0, 1):
+            for d in (1, -1):
+                arrive(("q1", a, d), piece(a, -d, 0), turn(a, 0, -d))
+                lo = 0 if d == 1 else h // 2
+                send(("q1r", a, d), piece(a, -d, 0, lo, h // 2), piece(a, -d, 0, lo, h // 2), turn(a, 0, d))
+        for a in (0, 1):
+            for k in (-1, 1):
+                for d in (1, -1):
+                    send(("q2", a, k, d), piece(a, k, 0), piece(a, k, 0), turn(a, 1, d))
+
+    def p3():
+        for a in (0, 1):
+            for d in (1, -1):
+                lo = 0 if d == 1 else h // 2
+                arrive(("q1r", a, d), piece(a, -2 * d, 0, lo, h // 2), turn(a, 0, -d))
+            for d in (1, -1):
+                send(("q2", a, 2, d), piece(a, 2, 0), piece(a, 2, 0), turn(a, 1, d))
+
+    def relay(a, k, d):
+        arrive(("q2", a, k, d), piece(a, k, -d), turn(a, 1, -d))
+        if (k in (0, -1)) == (d == 1):
+            send(("q2r", a, k), piece(a, k, -d), piece(a, k, -d), turn(a, 1, d))
+
+    def p4():
+        for k in (0, -1, 1):
+            for a in (0, 1):
+                for d in (1, -1):
+                    relay(a, k, d)
+        arrive("y_far_up", grow_ref.at[line_at(c_of(-2), 0, h)], chip(dy=-1))
+        arrive("y_far_down", grow_ref.at[line_at(c_of(2), h, h)], chip(dy=1))
+        send(("c", 2), grow_ref.at[line_at(c_of(2))], grow_ref.at[line_at(c_of(2))], partner)
+
+    def p5():
+        for a in (0, 1):
+            for d in (1, -1):
+                relay(a, 2, d)
+
+    hooks = {(0, 0): p1, (0, 1): p2, (1, 0): p3, (1, 1): p4, (2, 0): p5}
+
+    arrive("s_back", s_out.at[pl.ds(other, half), :], partner)
+    invert_in(s_out, noise_ref, sinv_ref, hooks)
+
+    for key, _, dst, _, frm in halo:
+        arrive(key, dst, frm)
+    for d in (0, -1, 1, 2):
+        there = line_at(2 * step(y, d) + 1 - core)
+        arrive(("c", d), grow_ref.at[there], partner)
+    for a in (0, 1):
+        for k in (0, -1, 1, 2):
+            d = 1 if k in (0, -1) else -1
+            arrive(("q2r", a, k), piece(a, k, -2 * d), turn(a, 1, -d))
+    for c in sent:
+        c.wait_send()
+
+    @pl.when(jnp.logical_not(alone))
+    def _():
+        twin_copy.wait_send()
+
+
+def exchange(p, velf, vels, oi, oj, noise, wl, tile=256):
+    rows, cols = p.shape
+    count, cells = oi.shape[1], velf.shape[0]
+    half = count // 2
+    p1, p2 = half // RING, half // RING**2
     v = pl.BlockSpec(memory_space=pltpu.VMEM)
-    return pl.pallas_call(m_kernel, out_shape=jax.ShapeDtypeStruct(t.shape, F32), in_specs=[v] * 4, out_specs=v,
-        cost_estimate=pl.CostEstimate(flops=10**7, bytes_accessed=5 << 20, transcendentals=0))(wl, top, t, bot)
-
-
-def sides(block, axis, dim, width):
-    count = lax.axis_size(axis)
-    forward = [(i, i + 1) for i in range(count - 1)]
-    backward = [(target, source) for source, target in forward]
-    low = lax.ppermute(lax.slice_in_dim(block, block.shape[dim] - width, None, axis=dim), axis, forward)
-    high = lax.ppermute(lax.slice_in_dim(block, 0, width, axis=dim), axis, backward)
-    return low, high
+    hbm = pl.BlockSpec(memory_space=pl.ANY)
+    shape = lambda *s: jax.ShapeDtypeStruct(s, F32)
+    vmem = lambda *s: pltpu.VMEM(s, F32)
+    return pl.pallas_call(exchange_kernel,
+        out_shape=(shape(count, count), shape(rows, count), shape(cols, count), shape(cells, cols), shape(cells, cols),
+                   shape(rows + 2 * cells, cells), shape(rows + 2 * cells, cells)),
+        in_specs=[hbm, v, v, v, v, v, v],
+        out_specs=(v, v, v, hbm, hbm, hbm, hbm),
+        scratch_shapes=[
+            pltpu.VMEM((rows // tile, tile, cols), F32), pltpu.VMEM((cols, count), BF16), pltpu.VMEM((cols, count), BF16),
+            vmem(16, count), vmem(rows, count), vmem(count, count), vmem(2, cells, count),
+            vmem(rows // cells, cells, count), vmem(RING, cells, count), vmem(RING, cells, count),
+            vmem(2, cells // 2, count), vmem(2, cells, count),
+            vmem(count, count), vmem(half, count), vmem(2, 3, p1, half), vmem(2, 3, p2, half), vmem(2, 3, 8, 128),
+            vmem(count, count),
+            pltpu.SemaphoreType.DMA((rows // tile,)), pltpu.SemaphoreType.DMA((120,)), pltpu.SemaphoreType.DMA((120,))],
+        compiler_params=pltpu.CompilerParams(vmem_limit_bytes=62 << 20, collective_id=0, has_side_effects=True),
+        cost_estimate=pl.CostEstimate(flops=12 * 10**9, bytes_accessed=20 << 20, transcendentals=0),
+    )(p, velf, vels, oi, oj, noise, wl)
 
 
 def cell_weights(vel_first, vel_second, start, lines):
     first = lax.dynamic_slice_in_dim(vel_first, start, lines, 0)
     second = lax.dynamic_slice_in_dim(vel_second, start, lines, 0)
+    line = lax.broadcasted_iota(jnp.int32, second.shape, 0) + start
     at = lax.broadcasted_iota(jnp.int32, second.shape, 1)
     ends = second.shape[1] - 1
     return [w.reshape(-1) for w in (
-        dispersion - 0.5 * first,
-        dispersion + 0.5 * first,
+        jnp.where(line == ends, 0.0, dispersion - 0.5 * first),
+        jnp.where(line == 0, 0.0, dispersion + 0.5 * first),
         jnp.where(at == ends, 0.0, dispersion - 0.5 * second),
         jnp.where(at == 0, 0.0, dispersion + 0.5 * second))]
 
@@ -280,34 +561,11 @@
     cells = vel_first.shape[0]
     row_lines, col_lines = rows // cells, cols // cells
     row_place, col_place = lax.axis_index("row"), lax.axis_index("col")
-    row_count, col_count = lax.axis_size("row"), lax.axis_size("col")
-    place = jnp.stack([row_place * row_lines, col_place * col_lines]).astype(jnp.int32)
     wl = jnp.stack(cell_weights(vel_first, vel_second, row_place * row_lines, row_lines), axis=1)
     wr = jnp.stack(cell_weights(vel_first, vel_second, col_place * col_lines, col_lines), axis=0)
     oi, oj = obs_cell[:, 0][None], obs_cell[:, 1][None]
-
-    t_part, s_part = partials(place, prior, vel_first, vel_second, oi, oj)
-    s_total = lax.psum(s_part, ("row", "col"))
-    t_top, t_bot = sides(t_part, "row", 0, cells)
-    g_part = sweep_panel(wl, t_top, t_part, t_bot)
-    g_line = lax.psum_scatter(g_part, "col", scatter_dimension=0, tiled=True)
-    blocks = cols // rows
-    perm = []
-    for r in range(row_count):
-        for c in range(col_count):
-            perm.append((r * col_count + c, ((r % blocks) * col_count + c) * col_count + r // blocks))
-    g_rows = lax.all_gather(g_line, "col", axis=0, tiled=True)
-    g_cols = lax.all_gather(lax.ppermute(g_line, ("row", "col"), perm), "row", axis=0, tiled=True)
-
-    lo, hi = sides(prior, "col", 1, cells)
-    top, bot = sides(prior, "row", 0, cells)
-    lo_top, lo_bot = sides(lo, "row", 0, cells)
-    hi_top, hi_bot = sides(hi, "row", 0, cells)
-    lo = jnp.concatenate([lo_top, lo, lo_bot], axis=0)
-    hi = jnp.concatenate([hi_top, hi, hi_bot], axis=0)
+    s_inv, g_rows, g_cols, top, bot, lo, hi = exchange(prior, vel_first, vel_second, oi, oj, obs_noise[None], wl)
     field = forecast(wl, wr, top, prior, bot, lo, hi, cells)
-
-    s_inv = invert(s_total + jnp.diag(obs_noise), 2, 128)
     return finish(field, g_rows, s_inv, g_cols, tile=512)
 
 

time: 321 us -> 172 us (0.54); the launches traced: 316 us -> 171 us
  waiting for transfers between devices: 146 us -> 0 us
  Pallas kernels: 88.3 us -> 158 us
  starting transfers between devices: 41.6 us -> 0 us
  between operations: 14.8 us -> 0.06 us
  local copies, waits for them, and re-layouts: 19.5 us -> 10.2 us
    psum x1 -> x0, waiting for transfers between devices: 95.2 us -> none  [body(): s_total = lax.psum(s_part, ('row', 'col'))]
    pallas_call x3 -> x1, Pallas kernels: 59.4 us -> 129 us  [exchange(): pl.pallas_call(exchange_kernel, out_shape=(shape(count, count), shape(row...]
    ppermute x11 -> x0, starting transfers between devices: 41.4 us -> none  [the longest x5 27.7 us: sides(): lax.ppermute(lax.slice_in_dim(block, block.shape[dim] - width, None, axis...]
    reduce_scatter x1 -> x0, waiting for transfers between devices: 37.5 us -> none  [body(): g_line = lax.psum_scatter(g_part, 'col', scatter_dimension=0, tiled=True)]
    ppermute x11 -> x0, waiting for transfers between devices: 13.2 us -> none  [the longest x1 7.67 us: body(): lax.ppermute(g_line, ('row', 'col'), perm)]
    slice x5 -> x0, local copies, waits for them, and re-layouts: 7.35 us -> none  [the longest x3 6.46 us: sides(): lax.slice_in_dim(block, 0, width, axis=dim)]
  transfers between devices with their start and end apart: 15 -> 0, of which waited for: 6 -> 0; matrix products, arithmetic and copies ran while one was open for 4% -> 0% of each run, Pallas kernels for 17% -> 0%
where the time goes in v2:
time: 172 us; the launch traced here: 171 us
  Pallas kernels  158 us (92%)
  local copies, waits for them, and re-layouts  10.2 us (6%)
  other arithmetic  3.01 us (2%)
    pallas_call x1, Pallas kernels, exchange(): pl.pallas_call(exchange_kernel, out_shape=(shape(count, count), shape(row...  129 us
    pallas_call x1, Pallas kernels, forecast(): pl.pallas_call(f_kernel, grid=(steps,), out_shape=jax.ShapeDtypeStruct((r...  14.8 us
    pallas_call x1, Pallas kernels, finish(): pl.pallas_call(fin_kernel, grid=(cols // tile,), out_shape=jax.ShapeDtype...  14.3 us
    unnamed x18, local copies, waits for them, and re-layouts  7.85 us

profile of v2, /device:TPU:1, one launch (start us, length us, event | category | flops | bytes accessed | tf_op | source)
XLA Modules:
  0.0 171.0 jit_solution(8730132829610375444)
XLA Ops:
  0.0 1.3 slice_bitcast_fusion
  1.4 0.8 subtract_select_fusion.3
  2.1 0.7 subtract_select_fusion.2
  2.9 0.7 subtract_select_fusion
  3.6 0.8 subtract_select_fusion.1
  4.4 1.0 copy.11.wl_ref
  5.4 0.0 copy-start.1
  5.4 128.5 %shard_map.55 = (f32[512,512]{1,0:T(8,128)}, f32[1024,512]{1,0:T(8,128)}, f32[2048,512]{1,0:T(8,128)}, f32[128,2048]{1,0:T(8,128)}, f32[128,2048]{1,0:T(8,128)},...) custom-call(f32[1024,2048]{1,0:T(8,128)} %p_next.1, f32[128,128]{1,0:T(8,128)} %velf_ref.1, f32[128,128]{1,0:T(8,128)} %vels_ref.1, ...), custom_call_target="tpu_custom_call" | custom-call | flops 12000000000 | bytes 20971520 | tf_op jit(solution)/shard_map/pallas_call | solution.py:528
  134.0 0.0 copy-done.1
  134.0 0.0 copy-start.2
  134.0 1.2 copy-done.2
  135.2 0.0 copy-start.3
  135.2 1.2 copy-done.3
  136.4 0.0 copy-start.4
  136.4 1.1 copy-done.4
  137.5 0.0 copy-start.5
  137.5 1.1 copy-done.5
  138.6 0.0 copy-start.6
  138.6 0.0 copy-start.7
  138.6 0.0 copy-start.8
  138.6 14.8 %shard_map.56.f_ref = f32[1024,2048]{1,0:T(8,128)S(1)} custom-call(f32[1024,4]{1,0:T(8,128)S(1)} %copy-done.1, f32[4,2048]{1,0:T(4,128)S(1)} %pad_maximum_fusion.wr_ref, f32[128,2048]{1,0:T(8,128)S(1)} %copy-done.2, f32[1024,2048]{1,0:T(8,128)} %p_next.1, f32[1024,2048]{1,0:T(8,128)} %p_next.1, f32[1024,2048]{1,0:T(8,128)} %p_next.1, ...), custom_call_target="tpu_custom_call" | custom-call | flops 50000000 | bytes 33554432 | tf_op jit(solution)/shard_map/pallas_call | solution.py:128
  153.5 0.0 copy-start
  153.5 3.2 %copy-done = f32[1024,2048]{1,0:T(8,128)} copy-done((f32[1024,2048]{1,0:T(8,128)}, f32[1024,2048]{1,0:T(8,128)S(1)}, u32[]{:S(2)}) %copy-start) | copy-done | bytes 8388632
  156.7 0.0 copy-done.6
  156.7 0.0 copy-done.7
  156.7 0.0 copy-done.8
  156.7 14.3 %shard_map.57 = f32[1024,2048]{1,0:T(8,128)} custom-call(f32[1024,2048]{1,0:T(8,128)} %copy-done, f32[1024,512]{1,0:T(8,128)S(1)} %copy-done.7, f32[512,512]{1,0:T(8,128)S(1)} %copy-done.8, f32[2048,512]{1,0:T(8,128)S(1)} %copy-done.6), custom_call_target="tpu_custom_call" | custom-call | flops 8000000000 | bytes 25165824 | tf_op jit(solution)/shard_map/pallas_call | solution.py:152
  (5 shorter events, 0.1 us)
Async XLA Ops:
  5.4 128.6 %copy-start.1 = (f32[1024,4]{1,0:T(8,128)S(1)}, f32[1024,4]{1,0:T(8,128)}, u32[]{:S(2)}) copy-start(f32[1024,4]{1,0:T(8,128)} %copy.11.wl_ref) | copy-start | bytes 49156
  134.0 1.2 copy-start.2
  135.2 1.2 copy-start.3
  136.4 1.1 copy-start.4
  137.5 1.1 copy-start.5
  138.6 18.1 %copy-start.6 = (f32[2048,512]{1,0:T(8,128)S(1)}, f32[2048,512]{1,0:T(8,128)}, u32[]{:S(2)}) copy-start(f32[2048,512]{1,0:T(8,128)} %get-tuple-element.18.gc_ref) | copy-start | bytes 12582916
  138.6 18.1 %copy-start.7 = (f32[1024,512]{1,0:T(8,128)S(1)}, f32[1024,512]{1,0:T(8,128)}, u32[]{:S(2)}) copy-start(f32[1024,512]{1,0:T(8,128)} %get-tuple-element.16.g_ref) | copy-start | bytes 6291460
  138.6 18.1 %copy-start.8 = (f32[512,512]{1,0:T(8,128)S(1)}, f32[512,512]{1,0:T(8,128)}, u32[]{:S(2)}) copy-start(f32[512,512]{1,0:T(8,128)} %get-tuple-element.17.s_ref) | copy-start | bytes 3145732
  153.5 3.2 %copy-start = (f32[1024,2048]{1,0:T(8,128)}, f32[1024,2048]{1,0:T(8,128)S(1)}, u32[]{:S(2)}) copy-start(f32[1024,2048]{1,0:T(8,128)S(1)} %shard_map.56.f_ref) | copy-start | bytes 25165828

commit v3 on v2

v3 whole, which is shorter than its diff:
```python
import functools
import jax
import jax.numpy as jnp
from jax import lax
from jax.experimental import pallas as pl
from jax.experimental.pallas import tpu as pltpu
from jax.sharding import PartitionSpec as P

HI = lax.Precision.HIGHEST
F32, BF16 = jnp.float32, jnp.bfloat16
dispersion = 0.125
centre_weight = 1.0 - 4.0 * dispersion
interp_weights = (0.42, 0.28, 0.18, 0.12)

def split(x):
    hi = x.astype(BF16)
    return hi, (x - hi.astype(F32)).astype(BF16)

def dot3(a, b, dims):
    (ah, al), (bh, bl) = a, b
    dg = functools.partial(lax.dot_general, dimension_numbers=(dims, ((), ())), preferred_element_type=F32)
    return dg(ah, bh) + (dg(ah, bl) + dg(al, bh))

def observed_weights(velf_ref, vels_ref, oi, oj):
    cells, count = velf_ref.shape[0], oi.shape[1]
    cid = lax.broadcasted_iota(jnp.int32, (cells, count), 0)
    w = {}
    def add(di, dj, v):
        w[di, dj] = w[di, dj] + v if (di, dj) in w else v
    for a in (0, 1):
        pick = jnp.where(cid == oi + a, 1.0, 0.0).astype(F32)
        by_j = [lax.dot_general(v[...], pick, (((0,), (0,)), ((), ())), precision=HI, preferred_element_type=F32)
                for v in (velf_ref, vels_ref)]
        for b in (0, 1):
            here = cid == oj + b
            vf, vs = [jnp.sum(jnp.where(here, x, 0.0), axis=0, keepdims=True) for x in by_j]
            h = interp_weights[2 * a + b]
            add(a, b, jnp.full_like(vf, h * centre_weight))
            add(a + 1, b, h * (dispersion - 0.5 * vf))
            add(a - 1, b, h * (dispersion + 0.5 * vf))
            add(a, b + 1, h * (dispersion - 0.5 * vs))
            add(a, b - 1, h * (dispersion + 0.5 * vs))
    return w

def line_weights(w, oi, oj, line, cells):
    count = oi.shape[1]
    jid = lax.broadcasted_iota(jnp.int32, (cells, count), 0)
    out = jnp.zeros((cells, count), F32)
    for dj in (-1, 0, 1, 2):
        row = jnp.zeros((1, count), F32)
        for di in (-1, 0, 1, 2):
            if (di, dj) in w:
                row = row + jnp.where(oi + di == line, w[di, dj], 0.0)
        out = jnp.where(jid == oj + dj, row, out)
    return out


def observed_panel(first_row, first_col, fetch, velf_ref, vels_ref, obs_ref, ext, t_ext, s_ref, ch, cl, wsc):
    cells = velf_ref.shape[0]
    lines, cols = ext.shape[0] - 2, ext.shape[2] - 2 * cells
    w = observed_weights(velf_ref, vels_ref, obs_ref[0:1, :], obs_ref[1:2, :])
    keys = sorted(w)
    for n, key in enumerate(keys):
        wsc[n:n + 1, :] = w[key]

    def at_line(line):
        table = {key: wsc[n:n + 1, :] for n, key in enumerate(keys)}
        return line_weights(table, obs_ref[0:1, :], obs_ref[1:2, :], line, cells)

    def build(l, _):
        at = pl.ds(pl.multiple_of(l * cells, cells), cells)
        ch[at, :], cl[at, :] = split(at_line(first_col + l))
        return 0
    lax.fori_loop(0, cols // cells, build, 0)
    s_ref[...] = jnp.zeros_like(s_ref)
    take = 2

    def run(n, _):
        for m in range(take):
            fetch(n * take + m).wait()
        at = pl.ds(1 + n * take, take)
        p = ext[at, :, cells:cells + cols].reshape(take * cells, cols)
        t = dot3(split(p), (ch[...], cl[...]), ((1,), (0,)))
        t_ext[at] = t.reshape(take, cells, t.shape[1])
        c = jnp.concatenate([at_line(first_row + n * take + m) for m in range(take)], axis=0)
        s_ref[...] += dot3(split(c), split(t), ((0,), (0,)))
        return 0
    lax.fori_loop(0, lines // take, run, 0)


def left_sweep(prev, mid, nxt, w):
    cells = mid.shape[0]
    up = pltpu.roll(mid, cells - 1, 0)
    down = pltpu.roll(mid, 1, 0)
    return centre_weight * mid + w[0] * nxt + w[1] * prev + w[2] * up + w[3] * down


def stencil_tables(velf_ref, vels_ref, first_row, first_col, wl, wr):
    cells = velf_ref.shape[0]
    by_first, by_second = velf_ref[...].T, vels_ref[...].T
    rid = lax.broadcasted_iota(jnp.int32, (cells, cells), 0)
    cid = lax.broadcasted_iota(jnp.int32, (cells, cells), 1)
    ends = cells - 1

    def row_line(l, _):
        line = first_row + l
        here = cid == line
        a, b = [jnp.broadcast_to(jnp.sum(jnp.where(here, v, 0.0), axis=1, keepdims=True), (cells, cells))
                for v in (by_first, by_second)]
        wl[l, 0] = jnp.where(line == ends, 0.0, dispersion - 0.5 * a)
        wl[l, 1] = jnp.where(line == 0, 0.0, dispersion + 0.5 * a)
        wl[l, 2] = jnp.where(rid == ends, 0.0, dispersion - 0.5 * b)
        wl[l, 3] = jnp.where(rid == 0, 0.0, dispersion + 0.5 * b)
        return 0
    lax.fori_loop(0, wl.shape[0], row_line, 0)

    def col_line(l, _):
        line = first_col + l
        a, b = velf_ref[pl.ds(line, 1), :], vels_ref[pl.ds(line, 1), :]
        lane = cid[:1]
        wr[l, 0:1, :] = jnp.where(line == ends, 0.0, dispersion - 0.5 * a)
        wr[l, 1:2, :] = jnp.where(line == 0, 0.0, dispersion + 0.5 * a)
        wr[l, 2:3, :] = jnp.where(lane == ends, 0.0, dispersion - 0.5 * b)
        wr[l, 3:4, :] = jnp.where(lane == 0, 0.0, dispersion + 0.5 * b)
        return 0
    lax.fori_loop(0, wr.shape[0], col_line, 0)


def forecast_line(i, ext, wl, wr, q_ref, f_ref):
    cells = ext.shape[1]
    spans = q_ref.shape[0]

    def rows_of(l):
        s = pl.ds(pl.multiple_of(l * cells, cells), cells)
        w = [wl[i, m] for m in range(4)]
        q_ref[l] = left_sweep(ext[i, :, s], ext[i + 1, :, s], ext[i + 2, :, s], w)

    def cols_of(l):
        s = pl.ds(pl.multiple_of(l * cells, cells), cells)
        mid = q_ref[l + 1]
        f_ref[i, :, s] = (centre_weight * mid + wr[l, 0:1, :] * q_ref[l + 2] + wr[l, 1:2, :] * q_ref[l]
                          + wr[l, 2:3, :] * pltpu.roll(mid, cells - 1, 1) + wr[l, 3:4, :] * pltpu.roll(mid, 1, 1))

    def pair(f):
        def run(n, _):
            f(2 * n)
            f(2 * n + 1)
            return 0
        return run
    lax.fori_loop(0, spans // 2, pair(rows_of), 0)
    lax.fori_loop(0, spans // 2 - 1, pair(cols_of), 0)


def fin_kernel(f_ref, g_ref, s_ref, gc_ref, o_ref, wh, wlo):
    @pl.when(pl.program_id(0) == 0)
    def _():
        w = jnp.dot(g_ref[...], s_ref[...], precision=HI, preferred_element_type=F32)
        h, l = split(w)
        wh[...] = h
        wlo[...] = l
    o_ref[...] = f_ref[...] - dot3((wh[...], wlo[...]), split(gc_ref[...]), ((1,), (1,)))

def finish(f, g, s, gc, tile=256):
    rows, cols = f.shape
    count = s.shape[0]
    whole = lambda x: pl.BlockSpec(x.shape, lambda n: (0, 0), pipeline_mode=pl.Buffered(1))
    return pl.pallas_call(fin_kernel, grid=(cols // tile,),
        out_shape=jax.ShapeDtypeStruct((rows, cols), F32),
        in_specs=[pl.BlockSpec((rows, tile), lambda n: (0, n)), whole(g), whole(s), pl.BlockSpec((tile, count), lambda n: (n, 0))],
        out_specs=pl.BlockSpec((rows, tile), lambda n: (0, n)),
        scratch_shapes=[pltpu.VMEM((rows, count), BF16), pltpu.VMEM((rows, count), BF16)],
        compiler_params=pltpu.CompilerParams(vmem_limit_bytes=40 << 20),
        cost_estimate=pl.CostEstimate(flops=8 * 10**9, bytes_accessed=24 << 20, transcendentals=0),
    )(f, g, s, gc)


def invert_in(s_ref, noise_ref, o_ref, hooks, block=128, parts=4):
    n = s_ref.shape[0]
    s = s_ref[...]
    rid = lax.broadcasted_iota(jnp.int32, (n, n), 0)
    cid = lax.broadcasted_iota(jnp.int32, (n, n), 1)
    o_ref[...] = 0.5 * (s + s.T) + jnp.where(rid == cid, noise_ref[...], 0.0)
    nb = n // block
    for k in range(nb):
        own = slice(k * block, (k + 1) * block)
        a = o_ref[own, own]
        for part in range(parts):
            for hook in hooks.get((k, part), ()):
                hook()
            a = pivot(a, range(part * block // parts, (part + 1) * block // parts, 4))
        panel = jnp.dot(a, o_ref[own, :], precision=HI, preferred_element_type=F32)
        col = o_ref[:, own]
        for j in range(nb):
            here = slice(j * block, (j + 1) * block)
            r = a if j == k else panel[:, here]
            upd = jnp.dot(col, r, precision=HI, preferred_element_type=F32)
            o_ref[:, here] = -upd if j == k else o_ref[:, here] - upd
            o_ref[own, here] = r


def pivot(a, steps):
    rid = lax.broadcasted_iota(jnp.int32, a.shape, 0)
    cid = lax.broadcasted_iota(jnp.int32, a.shape, 1)
    lane = cid[:1]
    four = range(4)
    for k in steps:
        col = [jnp.broadcast_to(a[:, k + j:k + j + 1], a.shape) for j in four]
        p = {(i, j): col[j][k + i:k + i + 1, :] for j in four for i in range(j + 1)}
        inside = (lane >= k) & (lane < k + 4)
        row = [jnp.where(inside, jnp.where(lane == k + j, 1.0, 0.0), a[k + j:k + j + 1, :]) for j in four]
        det = 1.0 / (p[0, 0] * p[1, 1] - p[0, 1] * p[0, 1])
        a00, a01, a11 = p[1, 1] * det, -p[0, 1] * det, p[0, 0] * det
        x00, x01 = a00 * p[0, 2] + a01 * p[1, 2], a00 * p[0, 3] + a01 * p[1, 3]
        x10, x11 = a01 * p[0, 2] + a11 * p[1, 2], a01 * p[0, 3] + a11 * p[1, 3]
        s22 = p[2, 2] - (p[0, 2] * x00 + p[1, 2] * x10)
        s23 = p[2, 3] - (p[0, 2] * x01 + p[1, 2] * x11)
        s33 = p[3, 3] - (p[0, 3] * x01 + p[1, 3] * x11)
        u0, u1 = a00 * row[0] + a01 * row[1], a01 * row[0] + a11 * row[1]
        v2 = row[2] - (x00 * row[0] + x10 * row[1])
        v3 = row[3] - (x01 * row[0] + x11 * row[1])
        det = 1.0 / (s22 * s33 - s23 * s23)
        r2, r3 = (s33 * v2 - s23 * v3) * det, (s22 * v3 - s23 * v2) * det
        r0, r1 = u0 - (x00 * r2 + x01 * r3), u1 - (x10 * r2 + x11 * r3)
        base = jnp.where((cid >= k) & (cid < k + 4), 0.0, a)
        a = base - ((col[0] * r0 + col[1] * r1) + (col[2] * r2 + col[3] * r3))
        for j, r in enumerate((r0, r1, r2, r3)):
            a = jnp.where(rid == k + j, r, a)
    return a


MESH = pl.DeviceIdType.MESH
RING = 4


def exchange_kernel(p_hbm, velf_ref, vels_ref, obs_ref, noise_ref,
                    sinv_ref, grow_ref, gcol_ref, f_hbm,
                    ext, ch, cl, wsc, wl, wr, q_ref, f_ref, t_ext, s_ref, gp, rg, gs, ry, rl,
                    s_acc, r0, r1, r2, r3, s_out, in_sems, out_sems, send_sems, recv_sems):
    lines, cells, cols = p_hbm.shape
    count = obs_ref.shape[1]
    row, col = lax.axis_index("row"), lax.axis_index("col")
    row_count, col_count = lax.axis_size("row"), lax.axis_size("col")
    x, z = row // RING, row % RING
    y, core = col // 2, col % 2
    col_lines = cols // cells
    inner = pl.ds(cells, cols)

    def fetch(n):
        return pltpu.make_async_copy(p_hbm.at[n], ext.at[n + 1, :, inner], in_sems.at[n])

    for n in range(lines):
        fetch(n).start()

    def step(v, d):
        return (v + d + RING) % RING

    def chip(dx=0, dy=0, dz=0):
        return (step(x, dx) * RING + step(z, dz), step(y, dy) * 2 + core)

    partner = (row, col + 1 - 2 * core)
    twin_row = y * RING + 2 * core + z % 2
    twin_col = 2 * x + z // 2
    twin = (twin_row, twin_col)
    alone = (twin_row == row) & (twin_col == col)
    up, down = (row + 1) % row_count, (row + row_count - 1) % row_count
    right, left = (col + 1) % col_count, (col + col_count - 1) % col_count

    barrier = pltpu.get_barrier_semaphore()
    greeted = [partner, (up, col), (down, col), (row, right), (row, left),
               (up, right), (up, left), (down, right), (down, left)]
    greeted += [chip(dx=d) for d in (1, 2, 3)] + [chip(dy=d) for d in (1, 2, 3)] + [chip(dz=d) for d in (1, 2, 3)]
    for peer in greeted:
        pl.semaphore_signal(barrier, inc=1, device_id=peer, device_id_type=MESH)

    @pl.when(jnp.logical_not(alone))
    def _():
        pl.semaphore_signal(barrier, inc=1, device_id=twin, device_id_type=MESH)
    pl.semaphore_wait(barrier, len(greeted) + 1 - alone.astype(jnp.int32))

    used, sent = {}, []

    def slot(key):
        if key not in used:
            used[key] = len(used)
        return used[key]

    def copy(key, src, dst, peer):
        n = slot(key)
        return pltpu.make_async_remote_copy(src_ref=src, dst_ref=dst, send_sem=send_sems.at[n], recv_sem=recv_sems.at[n],
                                            device_id=peer, device_id_type=MESH)

    def send(key, src, dst, peer):
        c = copy(key, src, dst, peer)
        c.start()
        sent.append(c)

    def arrive(key, dst, peer):
        copy(key, dst, dst, peer).wait_recv()

    low, high = pl.ds(0, cells), pl.ds(cols + cells, cells)
    head, tail = pl.ds(0, cells), pl.ds(cols - cells, cells)
    top, bot = 0, lines + 1
    late = cols // 4
    block = pl.ds(1, lines)
    halo = [
        ("p_right", p_hbm.at[:, :, tail], ext.at[block, :, low], (row, right), (row, left)),
        ("p_left", p_hbm.at[:, :, head], ext.at[block, :, high], (row, left), (row, right)),
        ("p_up_right", p_hbm.at[lines - 1, :, tail], ext.at[top, :, low], (up, right), (down, left)),
        ("p_up_left", p_hbm.at[lines - 1, :, head], ext.at[top, :, high], (up, left), (down, right)),
        ("p_down_right", p_hbm.at[0, :, tail], ext.at[bot, :, low], (down, right), (up, left)),
        ("p_down_left", p_hbm.at[0, :, head], ext.at[bot, :, high], (down, left), (up, right)),
        ("p_up", p_hbm.at[lines - 1, :, pl.ds(late, cols - late)], ext.at[top, :, pl.ds(cells + late, cols - late)],
         (up, col), (down, col)),
        ("p_down", p_hbm.at[0, :, pl.ds(late, cols - late)], ext.at[bot, :, pl.ds(cells + late, cols - late)],
         (down, col), (up, col)),
        ("p_up_late", p_hbm.at[lines - 1, :, pl.ds(0, late)], ext.at[top, :, pl.ds(cells, late)], (up, col), (down, col)),
        ("p_down_late", p_hbm.at[0, :, pl.ds(0, late)], ext.at[bot, :, pl.ds(cells, late)], (down, col), (up, col)),
    ]
    for key, src, dst, to, _ in halo[:8]:
        send(key, src, dst, to)

    first_row, first_col = row * lines, col * col_lines
    stencil_tables(velf_ref, vels_ref, first_row, first_col, wl, wr)
    observed_panel(first_row, first_col, fetch, velf_ref, vels_ref, obs_ref, ext, t_ext, s_ref, ch, cl, wsc)

    def forecast_lines(start, stop):
        def one(i, _):
            forecast_line(i, ext, wl, wr, q_ref, f_ref)
            pltpu.make_async_copy(f_ref.at[i], f_hbm.at[i], out_sems.at[i]).start()
            return 0
        lax.fori_loop(start, stop, one, 0)

    send("t_up", t_ext.at[lines], t_ext.at[top], (up, col))
    send("t_down", t_ext.at[1], t_ext.at[bot], (down, col))
    half = count // 2
    mine = pl.multiple_of(core * half, half)
    other = pl.multiple_of(half - core * half, half)
    send("s_core", s_ref.at[pl.ds(other, half), :], r0.at[:, :], partner)
    for key, src, dst, to, _ in halo[8:]:
        send(key, src, dst, to)
    for key, _, dst, _, frm in halo[:2]:
        arrive(key, dst, frm)
    forecast_lines(1, 2)
    arrive("s_core", r0.at[:, :], partner)
    s_acc[pl.ds(mine, half), :] = s_ref[pl.ds(mine, half), :] + r0[...]

    wide = count // 2
    p1, p2 = half // RING, half // RING**2
    order = (("x", "y"), ("y", "x"))
    pos = {"x": x, "y": y, "z": z}

    def at1(a, i):
        return (pl.ds(pl.multiple_of(mine + i * p1, 8), p1), pl.ds(a * wide, wide))

    def at2(a, i, j):
        return (pl.ds(pl.multiple_of(mine + i * p1 + j * p2, 8), p2), pl.ds(a * wide, wide))

    def hop(axis, d):
        return chip(**{"d" + axis: d})

    def reduce_start(name, slots, place, axes):
        for a in (0, 1):
            for d in (1, 2, 3):
                axis = axes[a]
                send((name, a, d), s_acc.at[place(a, step(pos[axis], d))], slots.at[a, d - 1], hop(axis, d))

    def reduce_end(name, slots, place, axes):
        for a in (0, 1):
            for d in (1, 2, 3):
                arrive((name, a, d), slots.at[a, d - 1], hop(axes[a], -d))
            here = place(a, pos[axes[a]])
            s_acc[here] = (s_acc[here] + slots[a, 0]) + (slots[a, 1] + slots[a, 2])

    def gather_start(name, place, axes):
        for a in (0, 1):
            here = place(a, pos[axes[a]])
            for d in (1, 2, 3):
                send((name, a, d), s_out.at[here], s_out.at[here], hop(axes[a], d))

    def gather_end(name, place, axes):
        for a in (0, 1):
            for d in (1, 2, 3):
                there = place(a, step(pos[axes[a]], -d))
                arrive((name, a, d), s_out.at[there], hop(axes[a], -d))

    axes1, axes2 = [o[0] for o in order], [o[1] for o in order]
    own1 = [pos[a] for a in axes1]
    own2 = [pos[a] for a in axes2]
    place1 = at1
    place2 = lambda a, j: at2(a, own1[a], j)

    reduce_start("s1", r1, place1, axes1)

    forecast_lines(2, 4)

    arrive("t_up", t_ext.at[top], (down, col))
    arrive("t_down", t_ext.at[bot], (up, col))

    def sweep_line(l, _):
        w = [wl[l, m] for m in range(4)]
        for b in range(count // cells):
            s = slice(b * cells, (b + 1) * cells)
            gp[l, :, s] = left_sweep(t_ext[l, :, s], t_ext[l + 1, :, s], t_ext[l + 2, :, s], w)
        return 0
    lax.fori_loop(0, lines, sweep_line, 0)
    for q in range(RING):
        send(("g_core", q), gp.at[2 * q + 1 - core], rg.at[q], partner)

    reduce_end("s1", r1, place1, axes1)
    reduce_start("s2", r2, place2, axes2)

    for q in range(RING):
        arrive(("g_core", q), rg.at[q], partner)
        gs[q] = gp[2 * q + core] + rg[q]
    h = cells // 2
    first, second = pl.ds(0, h), pl.ds(h, h)
    far, nxt_y, prv_y = step(y, 2), step(y, 1), step(y, -1)
    send("g_far_up", gs.at[far, first], ry.at[0], chip(dy=1))
    send("g_far_down", gs.at[far, second], ry.at[1], chip(dy=-1))

    forecast_lines(4, 5)
    reduce_end("s2", r2, place2, axes2)
    for a in (0, 1):
        piece2 = s_acc.at[place2(a, own2[a])]
        for d in (1, 2, 3):
            send(("s3", a, d), piece2, r3.at[a, z], chip(dz=d))
        r3[a, z] = s_acc[place2(a, own2[a])]

    arrive("g_far_up", ry.at[0], chip(dy=-1))
    arrive("g_far_down", ry.at[1], chip(dy=1))
    gs[nxt_y, first] = gs[nxt_y, first] + ry[0]
    gs[prv_y, second] = gs[prv_y, second] + ry[1]
    send("g_up", gs.at[nxt_y], rl.at[0], chip(dy=1))
    send("g_down", gs.at[prv_y], rl.at[1], chip(dy=-1))

    forecast_lines(5, 6)
    for a in (0, 1):
        for d in (1, 2, 3):
            arrive(("s3", a, d), r3.at[a, step(z, -d)], chip(dz=-d))
        s_out[place2(a, own2[a])] = (r3[a, 0] + r3[a, 1]) + (r3[a, 2] + r3[a, 3])
    gather_start("a2", place2, axes2)
    forecast_lines(6, 7)
    gather_end("a2", place2, axes2)
    gather_start("a1", place1, axes1)

    arrive("g_up", rl.at[0], chip(dy=-1))
    arrive("g_down", rl.at[1], chip(dy=1))

    def line_at(c, lo=0, n=cells):
        return (pl.ds(pl.multiple_of(c * cells + lo, 8), n), slice(None))

    own = line_at(col)
    grow_ref[own] = (gs[y] + rl[0]) + rl[1]

    def col_line(xx, zz, lo=0, n=cells):
        return line_at(8 * (zz % 2) + 2 * xx + zz // 2, lo, n)

    landing = col_line(x, z)
    away = line_at(8 * (row % 2) + col)
    twin_copy = copy("twin", grow_ref.at[own], gcol_ref.at[away], twin)

    @pl.when(alone)
    def _():
        gcol_ref[landing] = grow_ref[own]

    @pl.when(jnp.logical_not(alone))
    def _():
        twin_copy.start()

    send("y_up", grow_ref.at[own], grow_ref.at[own], chip(dy=1))
    send("y_down", grow_ref.at[own], grow_ref.at[own], chip(dy=-1))
    send(("c", 0), grow_ref.at[own], grow_ref.at[own], partner)

    for key, _, dst, _, frm in halo[2:]:
        arrive(key, dst, frm)
    forecast_lines(0, 1)
    forecast_lines(7, 8)
    gather_end("a1", place1, axes1)
    whole = (pl.ds(mine, half), slice(None))
    send("s_back", s_out.at[whole], s_out.at[whole], partner)

    def c_of(d):
        return 2 * step(y, d) + core

    def twin_landed():
        @pl.when(jnp.logical_not(alone))
        def _():
            arrive("twin", gcol_ref.at[landing], twin)

    lows = (0, h)
    rings = (("x", "z"), ("z", "x"))

    def piece(a, d0, d1, lo=0, n=h):
        dx, dz = (d0, d1) if a == 0 else (d1, d0)
        return gcol_ref.at[col_line(step(x, dx), step(z, dz), lows[a] + lo, n)]

    def turn(a, level, d):
        return hop(rings[a][level], d)

    def p1():
        twin_landed()
        for a in (0, 1):
            for d in (1, -1):
                send(("q1", a, d), piece(a, 0, 0), piece(a, 0, 0), turn(a, 0, d))
        for a in (0, 1):
            for d in (1, -1):
                send(("q2", a, 0, d), piece(a, 0, 0), piece(a, 0, 0), turn(a, 1, d))
        arrive("y_up", grow_ref.at[line_at(c_of(-1))], chip(dy=-1))
        arrive("y_down", grow_ref.at[line_at(c_of(1))], chip(dy=1))
        send("y_far_up", grow_ref.at[line_at(c_of(-1), 0, h)], grow_ref.at[line_at(c_of(-1), 0, h)], chip(dy=1))
        send("y_far_down", grow_ref.at[line_at(c_of(1), h, h)], grow_ref.at[line_at(c_of(1), h, h)], chip(dy=-1))
        for d in (-1, 1):
            send(("c", d), grow_ref.at[line_at(c_of(d))], grow_ref.at[line_at(c_of(d))], partner)

    def p2():
        for a in (0, 1):
            for d in (1, -1):
                arrive(("q1", a, d), piece(a, -d, 0), turn(a, 0, -d))
                lo = 0 if d == 1 else h // 2
                send(("q1r", a, d), piece(a, -d, 0, lo, h // 2), piece(a, -d, 0, lo, h // 2), turn(a, 0, d))
        for a in (0, 1):
            for k in (-1, 1):
                for d in (1, -1):
                    send(("q2", a, k, d), piece(a, k, 0), piece(a, k, 0), turn(a, 1, d))

    def p3():
        for a in (0, 1):
            for d in (1, -1):
                lo = 0 if d == 1 else h // 2
                arrive(("q1r", a, d), piece(a, -2 * d, 0, lo, h // 2), turn(a, 0, -d))
            for d in (1, -1):
                send(("q2", a, 2, d), piece(a, 2, 0), piece(a, 2, 0), turn(a, 1, d))

    def relay(a, k, d):
        arrive(("q2", a, k, d), piece(a, k, -d), turn(a, 1, -d))
        if (k in (0, -1)) == (d == 1):
            send(("q2r", a, k), piece(a, k, -d), piece(a, k, -d), turn(a, 1, d))

    def relays(*ks):
        def run():
            for k in ks:
                for a in (0, 1):
                    for d in (1, -1):
                        relay(a, k, d)
        return run

    def p4():
        arrive("y_far_up", grow_ref.at[line_at(c_of(-2), 0, h)], chip(dy=-1))
        arrive("y_far_down", grow_ref.at[line_at(c_of(2), h, h)], chip(dy=1))
        send(("c", 2), grow_ref.at[line_at(c_of(2))], grow_ref.at[line_at(c_of(2))], partner)

    hooks = {(0, 2): [p1], (1, 1): [p2], (1, 3): [p3, relays(0)], (2, 2): [p4, relays(-1, 1)], (3, 1): [relays(2)]}

    arrive("s_back", s_out.at[pl.ds(other, half), :], partner)
    invert_in(s_out, noise_ref, sinv_ref, hooks)

    for d in (0, -1, 1, 2):
        there = line_at(2 * step(y, d) + 1 - core)
        arrive(("c", d), grow_ref.at[there], partner)
    for a in (0, 1):
        for k in (0, -1, 1, 2):
            d = 1 if k in (0, -1) else -1
            arrive(("q2r", a, k), piece(a, k, -2 * d), turn(a, 1, -d))
    for c in sent:
        c.wait_send()
    for n in range(lines):
        pltpu.make_async_copy(f_ref.at[n], f_hbm.at[n], out_sems.at[n]).wait()

    @pl.when(jnp.logical_not(alone))
    def _():
        twin_copy.wait_send()


def exchange(p, velf, vels, obs, noise):
    rows, cols = p.shape
    count, cells = obs.shape[1], velf.shape[0]
    lines = rows // cells
    half = count // 2
    p1, p2 = half // RING, half // RING**2
    v = pl.BlockSpec(memory_space=pltpu.VMEM)
    hbm = pl.BlockSpec(memory_space=pl.ANY)
    shape = lambda *s: jax.ShapeDtypeStruct(s, F32)
    vmem = lambda *s: pltpu.VMEM(s, F32)
    return pl.pallas_call(exchange_kernel,
        out_shape=(shape(count, count), shape(rows, count), shape(cols, count), shape(lines, cells, cols)),
        in_specs=[hbm, v, v, v, v],
        out_specs=(v, v, v, hbm),
        scratch_shapes=[
            vmem(lines + 2, cells, cols + 2 * cells), pltpu.VMEM((cols, count), BF16), pltpu.VMEM((cols, count), BF16),
            vmem(16, count), vmem(lines, 4, cells, cells), vmem(cols // cells, 8, cells), vmem(cols // cells + 2, cells, cells),
            vmem(lines, cells, cols), vmem(lines + 2, cells, count), vmem(count, count),
            vmem(lines, cells, count), vmem(RING, cells, count), vmem(RING, cells, count),
            vmem(2, cells // 2, count), vmem(2, cells, count),
            vmem(count, count), vmem(half, count), vmem(2, 3, p1, half), vmem(2, 3, p2, half), vmem(2, RING, p2, half),
            vmem(count, count),
            pltpu.SemaphoreType.DMA((lines,)), pltpu.SemaphoreType.DMA((lines,)),
            pltpu.SemaphoreType.DMA((100,)), pltpu.SemaphoreType.DMA((100,))],
        compiler_params=pltpu.CompilerParams(vmem_limit_bytes=62 << 20, collective_id=0, has_side_effects=True),
        cost_estimate=pl.CostEstimate(flops=12 * 10**9, bytes_accessed=28 << 20, transcendentals=0),
    )(p.reshape(lines, cells, cols), velf, vels, obs, noise)


def body(prior, vel_first, vel_second, obs_cell, obs_noise):
    s_inv, g_rows, g_cols, field = exchange(prior, vel_first, vel_second, obs_cell.T, obs_noise[None])
    return finish(field.reshape(prior.shape), g_rows, s_inv, g_cols, tile=512)


def solution(mesh):
    placed = (P("row", "col"), P(), P(), P(), P())
    return jax.shard_map(body, mesh=mesh, in_specs=placed, out_specs=P("row", "col"), check_vma=False)
```

time: 172 us -> 135 us (0.78)
  Pallas kernels: 158 us -> 129 us
  local copies, waits for them, and re-layouts: 10.2 us -> 5 us
  other arithmetic: 3.01 us -> 0 us
    pallas_call x1 -> x0, Pallas kernels: 14.8 us -> none  [forecast(): pl.pallas_call(f_kernel, grid=(steps,), out_shape=jax.ShapeDtypeStruct((r...]
    pallas_call x1, Pallas kernels: 129 us -> 115 us  [exchange(): pl.pallas_call(exchange_kernel, out_shape=(shape(count, count), shape(row...]
    select_n x4 -> x0, other arithmetic: 2.93 us -> none  [the longest x2 1.53 us: cell_weights(): jnp.where(line == ends, 0.0, dispersion - 0.5 * first)]
    unnamed x18 -> x6, local copies, waits for them, and re-layouts: 7.85 us -> 5 us
    another operation x2 -> x0, local copies, waits for them, and re-layouts: 2.37 us -> none  [the longest x1 1.35 us: body(): oi, oj = (obs_cell[:, 0][None], obs_cell[:, 1][None])]
where the time goes in v3:
time: 135 us; the launch traced here: 134 us
  Pallas kernels  129 us (96%)
  local copies, waits for them, and re-layouts  5 us (4%)
    pallas_call x1, Pallas kernels, exchange(): pl.pallas_call(exchange_kernel, out_shape=(shape(count, count), shape(row...  115 us
    pallas_call x1, Pallas kernels, finish(): pl.pallas_call(fin_kernel, grid=(cols // tile,), out_shape=jax.ShapeDtype...  14.3 us
    unnamed x6, local copies, waits for them, and re-layouts  5 us

profile of v3, /device:TPU:1, one launch (start us, length us, event | category | flops | bytes accessed | tf_op | source)
XLA Modules:
  0.0 134.3 jit_solution(12119857147518927454)
XLA Ops:
  0.0 114.9 %shard_map.55 = (f32[512,512]{1,0:T(8,128)}, f32[1024,512]{1,0:T(8,128)}, f32[2048,512]{1,0:T(8,128)}, f32[8,128,2048]{2,1,0:T(8,128)}) custom-call(f32[8,128,2048]{2,1,0:T(8,128)} %bitcast.4, f32[128,128]{1,0:T(8,128)} %velf_ref.1, f32[128,128]{1,0:T(8,128)} %vels_ref.1, s32[2,512]{1,0:T(2,128)} %bitcast.5, f32[1,512]{1,0:T(1,128)} %bitcast.6), custom_call_target="tpu_custom_call" | custom-call | flops 12000000000 | bytes 29360128 | tf_op jit(solution)/shard_map/pallas_call | solution.py:584
  114.9 0.0 copy-start
  115.0 2.2 %copy-done = f32[2048,512]{1,0:T(8,128)S(1)} copy-done((f32[2048,512]{1,0:T(8,128)S(1)}, f32[2048,512]{1,0:T(8,128)}, u32[]{:S(2)}) %copy-start) | copy-done | bytes 4194328
  117.1 0.0 copy-start.1
  117.1 1.6 %copy-done.1 = f32[1024,512]{1,0:T(8,128)S(1)} copy-done((f32[1024,512]{1,0:T(8,128)S(1)}, f32[1024,512]{1,0:T(8,128)}, u32[]{:S(2)}) %copy-start.1) | copy-done | bytes 2097176
  118.7 0.0 copy-start.2
  118.7 1.2 copy-done.2
  119.9 14.3 %shard_map.56 = f32[1024,2048]{1,0:T(8,128)} custom-call(f32[1024,2048]{1,0:T(8,128)} %bitcast.7, f32[1024,512]{1,0:T(8,128)S(1)} %copy-done.1, f32[512,512]{1,0:T(8,128)S(1)} %copy-done.2, f32[2048,512]{1,0:T(8,128)S(1)} %copy-done), custom_call_target="tpu_custom_call" | custom-call | flops 8000000000 | bytes 25165824 | tf_op jit(solution)/shard_map/pallas_call | solution.py:167
Async XLA Ops:
  114.9 2.2 %copy-start = (f32[2048,512]{1,0:T(8,128)S(1)}, f32[2048,512]{1,0:T(8,128)}, u32[]{:S(2)}) copy-start(f32[2048,512]{1,0:T(8,128)} %get-tuple-element.12.gc_ref) | copy-start | bytes 12582916
  117.1 1.6 %copy-start.1 = (f32[1024,512]{1,0:T(8,128)S(1)}, f32[1024,512]{1,0:T(8,128)}, u32[]{:S(2)}) copy-start(f32[1024,512]{1,0:T(8,128)} %get-tuple-element.10.g_ref) | copy-start | bytes 6291460
  118.7 1.2 copy-start.2

commit v4 on v3

--- a/solution.py
+++ b/solution.py
@@ -55,7 +55,7 @@
     return out
 
 
-def observed_panel(first_row, first_col, fetch, velf_ref, vels_ref, obs_ref, ext, t_ext, s_ref, ch, cl, wsc):
+def observed_panel(first_row, first_col, fetch, velf_ref, vels_ref, obs_ref, ext, t_ext, s_ref, ch, cl, wsc, send_edges):
     cells = velf_ref.shape[0]
     lines, cols = ext.shape[0] - 2, ext.shape[2] - 2 * cells
     w = observed_weights(velf_ref, vels_ref, obs_ref[0:1, :], obs_ref[1:2, :])
@@ -85,7 +85,10 @@
         c = jnp.concatenate([at_line(first_row + n * take + m) for m in range(take)], axis=0)
         s_ref[...] += dot3(split(c), split(t), ((0,), (0,)))
         return 0
-    lax.fori_loop(0, lines // take, run, 0)
+    last = lines // take - 1
+    lax.fori_loop(0, 2, lambda n, _: run(n * last, _), 0)
+    send_edges()
+    lax.fori_loop(1, last, run, 0)
 
 
 def left_sweep(prev, mid, nxt, w):
@@ -151,27 +154,21 @@
     lax.fori_loop(0, spans // 2 - 1, pair(cols_of), 0)
 
 
-def fin_kernel(f_ref, g_ref, s_ref, gc_ref, o_ref, wh, wlo):
-    @pl.when(pl.program_id(0) == 0)
-    def _():
-        w = jnp.dot(g_ref[...], s_ref[...], precision=HI, preferred_element_type=F32)
-        h, l = split(w)
-        wh[...] = h
-        wlo[...] = l
-    o_ref[...] = f_ref[...] - dot3((wh[...], wlo[...]), split(gc_ref[...]), ((1,), (1,)))
-
-def finish(f, g, s, gc, tile=256):
+def fin_kernel(f_ref, wh_ref, wlo_ref, gc_ref, o_ref):
+    o_ref[...] = f_ref[...] - dot3((wh_ref[...], wlo_ref[...]), split(gc_ref[...]), ((1,), (1,)))
+
+
+def finish(f, wh, wlo, gc, tile=512):
     rows, cols = f.shape
-    count = s.shape[0]
+    count = gc.shape[1]
     whole = lambda x: pl.BlockSpec(x.shape, lambda n: (0, 0), pipeline_mode=pl.Buffered(1))
     return pl.pallas_call(fin_kernel, grid=(cols // tile,),
         out_shape=jax.ShapeDtypeStruct((rows, cols), F32),
-        in_specs=[pl.BlockSpec((rows, tile), lambda n: (0, n)), whole(g), whole(s), pl.BlockSpec((tile, count), lambda n: (n, 0))],
+        in_specs=[pl.BlockSpec((rows, tile), lambda n: (0, n)), whole(wh), whole(wlo), pl.BlockSpec((tile, count), lambda n: (n, 0))],
         out_specs=pl.BlockSpec((rows, tile), lambda n: (0, n)),
-        scratch_shapes=[pltpu.VMEM((rows, count), BF16), pltpu.VMEM((rows, count), BF16)],
-        compiler_params=pltpu.CompilerParams(vmem_limit_bytes=40 << 20),
+        compiler_params=pltpu.CompilerParams(vmem_limit_bytes=62 << 20),
         cost_estimate=pl.CostEstimate(flops=8 * 10**9, bytes_accessed=24 << 20, transcendentals=0),
-    )(f, g, s, gc)
+    )(f, wh, wlo, gc)
 
 
 def invert_in(s_ref, noise_ref, o_ref, hooks, block=128, parts=4):
@@ -233,9 +230,9 @@
 
 
 def exchange_kernel(p_hbm, velf_ref, vels_ref, obs_ref, noise_ref,
-                    sinv_ref, grow_ref, gcol_ref, f_hbm,
+                    wh_ref, wlo_ref, gcol_ref, f_hbm,
                     ext, ch, cl, wsc, wl, wr, q_ref, f_ref, t_ext, s_ref, gp, rg, gs, ry, rl,
-                    s_acc, r0, r1, r2, r3, s_out, in_sems, out_sems, send_sems, recv_sems):
+                    s_acc, r0, r1, r2, r3, s_out, sinv_ref, grow_ref, in_sems, out_sems, twin_sem, send_sems, recv_sems):
     lines, cells, cols = p_hbm.shape
     count = obs_ref.shape[1]
     row, col = lax.axis_index("row"), lax.axis_index("col")
@@ -300,7 +297,7 @@
     low, high = pl.ds(0, cells), pl.ds(cols + cells, cells)
     head, tail = pl.ds(0, cells), pl.ds(cols - cells, cells)
     top, bot = 0, lines + 1
-    late = cols // 4
+    bounds = [cols * n // 16 for n in (0, 6, 8, 9, 10, 16)]
     block = pl.ds(1, lines)
     halo = [
         ("p_right", p_hbm.at[:, :, tail], ext.at[block, :, low], (row, right), (row, left)),
@@ -309,19 +306,29 @@
         ("p_up_left", p_hbm.at[lines - 1, :, head], ext.at[top, :, high], (up, left), (down, right)),
         ("p_down_right", p_hbm.at[0, :, tail], ext.at[bot, :, low], (down, right), (up, left)),
         ("p_down_left", p_hbm.at[0, :, head], ext.at[bot, :, high], (down, left), (up, right)),
-        ("p_up", p_hbm.at[lines - 1, :, pl.ds(late, cols - late)], ext.at[top, :, pl.ds(cells + late, cols - late)],
-         (up, col), (down, col)),
-        ("p_down", p_hbm.at[0, :, pl.ds(late, cols - late)], ext.at[bot, :, pl.ds(cells + late, cols - late)],
-         (down, col), (up, col)),
-        ("p_up_late", p_hbm.at[lines - 1, :, pl.ds(0, late)], ext.at[top, :, pl.ds(cells, late)], (up, col), (down, col)),
-        ("p_down_late", p_hbm.at[0, :, pl.ds(0, late)], ext.at[bot, :, pl.ds(cells, late)], (down, col), (up, col)),
     ]
-    for key, src, dst, to, _ in halo[:8]:
+    strips = []
+    for n, (lo, hi) in enumerate(zip(bounds[:-1], bounds[1:])):
+        src, dst = pl.ds(lo, hi - lo), pl.ds(cells + lo, hi - lo)
+        strips.append([
+            (("p_up", n), p_hbm.at[lines - 1, :, src], ext.at[top, :, dst], (up, col), (down, col)),
+            (("p_down", n), p_hbm.at[0, :, src], ext.at[bot, :, dst], (down, col), (up, col))])
+
+    def send_strip(n):
+        for key, src, dst, to, _ in strips[n]:
+            send(key, src, dst, to)
+
+    for key, src, dst, to, _ in halo:
         send(key, src, dst, to)
+    send_strip(0)
 
     first_row, first_col = row * lines, col * col_lines
     stencil_tables(velf_ref, vels_ref, first_row, first_col, wl, wr)
-    observed_panel(first_row, first_col, fetch, velf_ref, vels_ref, obs_ref, ext, t_ext, s_ref, ch, cl, wsc)
+    def send_edges():
+        send("t_up", t_ext.at[lines], t_ext.at[top], (up, col))
+        send("t_down", t_ext.at[1], t_ext.at[bot], (down, col))
+
+    observed_panel(first_row, first_col, fetch, velf_ref, vels_ref, obs_ref, ext, t_ext, s_ref, ch, cl, wsc, send_edges)
 
     def forecast_lines(start, stop):
         def one(i, _):
@@ -330,14 +337,10 @@
             return 0
         lax.fori_loop(start, stop, one, 0)
 
-    send("t_up", t_ext.at[lines], t_ext.at[top], (up, col))
-    send("t_down", t_ext.at[1], t_ext.at[bot], (down, col))
     half = count // 2
     mine = pl.multiple_of(core * half, half)
     other = pl.multiple_of(half - core * half, half)
     send("s_core", s_ref.at[pl.ds(other, half), :], r0.at[:, :], partner)
-    for key, src, dst, to, _ in halo[8:]:
-        send(key, src, dst, to)
     for key, _, dst, _, frm in halo[:2]:
         arrive(key, dst, frm)
     forecast_lines(1, 2)
@@ -390,8 +393,8 @@
     place2 = lambda a, j: at2(a, own1[a], j)
 
     reduce_start("s1", r1, place1, axes1)
-
-    forecast_lines(2, 4)
+    send_strip(1)
+
 
     arrive("t_up", t_ext.at[top], (down, col))
     arrive("t_down", t_ext.at[bot], (up, col))
@@ -405,9 +408,11 @@
     lax.fori_loop(0, lines, sweep_line, 0)
     for q in range(RING):
         send(("g_core", q), gp.at[2 * q + 1 - core], rg.at[q], partner)
+    forecast_lines(2, 3)
 
     reduce_end("s1", r1, place1, axes1)
     reduce_start("s2", r2, place2, axes2)
+    send_strip(2)
 
     for q in range(RING):
         arrive(("g_core", q), rg.at[q], partner)
@@ -418,7 +423,7 @@
     send("g_far_up", gs.at[far, first], ry.at[0], chip(dy=1))
     send("g_far_down", gs.at[far, second], ry.at[1], chip(dy=-1))
 
-    forecast_lines(4, 5)
+    forecast_lines(3, 4)
     reduce_end("s2", r2, place2, axes2)
     for a in (0, 1):
         piece2 = s_acc.at[place2(a, own2[a])]
@@ -426,22 +431,24 @@
             send(("s3", a, d), piece2, r3.at[a, z], chip(dz=d))
         r3[a, z] = s_acc[place2(a, own2[a])]
 
+    forecast_lines(4, 5)
+    for a in (0, 1):
+        for d in (1, 2, 3):
+            arrive(("s3", a, d), r3.at[a, step(z, -d)], chip(dz=-d))
+        s_out[place2(a, own2[a])] = (r3[a, 0] + r3[a, 1]) + (r3[a, 2] + r3[a, 3])
+    gather_start("a2", place2, axes2)
     arrive("g_far_up", ry.at[0], chip(dy=-1))
     arrive("g_far_down", ry.at[1], chip(dy=1))
     gs[nxt_y, first] = gs[nxt_y, first] + ry[0]
     gs[prv_y, second] = gs[prv_y, second] + ry[1]
     send("g_up", gs.at[nxt_y], rl.at[0], chip(dy=1))
     send("g_down", gs.at[prv_y], rl.at[1], chip(dy=-1))
-
+    send_strip(3)
     forecast_lines(5, 6)
-    for a in (0, 1):
-        for d in (1, 2, 3):
-            arrive(("s3", a, d), r3.at[a, step(z, -d)], chip(dz=-d))
-        s_out[place2(a, own2[a])] = (r3[a, 0] + r3[a, 1]) + (r3[a, 2] + r3[a, 3])
-    gather_start("a2", place2, axes2)
-    forecast_lines(6, 7)
     gather_end("a2", place2, axes2)
     gather_start("a1", place1, axes1)
+    send_strip(4)
+    forecast_lines(6, 7)
 
     arrive("g_up", rl.at[0], chip(dy=-1))
     arrive("g_down", rl.at[1], chip(dy=1))
@@ -461,7 +468,7 @@
 
     @pl.when(alone)
     def _():
-        gcol_ref[landing] = grow_ref[own]
+        pltpu.make_async_copy(grow_ref.at[own], gcol_ref.at[landing], twin_sem).start()
 
     @pl.when(jnp.logical_not(alone))
     def _():
@@ -471,10 +478,6 @@
     send("y_down", grow_ref.at[own], grow_ref.at[own], chip(dy=-1))
     send(("c", 0), grow_ref.at[own], grow_ref.at[own], partner)
 
-    for key, _, dst, _, frm in halo[2:]:
-        arrive(key, dst, frm)
-    forecast_lines(0, 1)
-    forecast_lines(7, 8)
     gather_end("a1", place1, axes1)
     whole = (pl.ds(mine, half), slice(None))
     send("s_back", s_out.at[whole], s_out.at[whole], partner)
@@ -486,6 +489,10 @@
         @pl.when(jnp.logical_not(alone))
         def _():
             arrive("twin", gcol_ref.at[landing], twin)
+
+        @pl.when(alone)
+        def _():
+            pltpu.make_async_copy(grow_ref.at[own], gcol_ref.at[landing], twin_sem).wait()
 
     lows = (0, h)
     rings = (("x", "z"), ("z", "x"))
@@ -549,7 +556,13 @@
         arrive("y_far_down", grow_ref.at[line_at(c_of(2), h, h)], chip(dy=1))
         send(("c", 2), grow_ref.at[line_at(c_of(2))], grow_ref.at[line_at(c_of(2))], partner)
 
-    hooks = {(0, 2): [p1], (1, 1): [p2], (1, 3): [p3, relays(0)], (2, 2): [p4, relays(-1, 1)], (3, 1): [relays(2)]}
+    def edge_lines():
+        for key, _, dst, _, frm in halo[2:] + sum(strips, []):
+            arrive(key, dst, frm)
+        forecast_lines(0, 1)
+        forecast_lines(lines - 1, lines)
+
+    hooks = {(0, 2): [p1], (1, 1): [edge_lines, p2], (1, 3): [p3, relays(0)], (2, 2): [p4, relays(-1, 1)], (3, 1): [relays(2)]}
 
     arrive("s_back", s_out.at[pl.ds(other, half), :], partner)
     invert_in(s_out, noise_ref, sinv_ref, hooks)
@@ -557,6 +570,13 @@
     for d in (0, -1, 1, 2):
         there = line_at(2 * step(y, d) + 1 - core)
         arrive(("c", d), grow_ref.at[there], partner)
+
+    def update_rows(n, _):
+        at = pl.ds(pl.multiple_of(n * 2 * cells, 2 * cells), 2 * cells)
+        w = jnp.dot(grow_ref[at, :], sinv_ref[...], precision=HI, preferred_element_type=F32)
+        wh_ref[at, :], wlo_ref[at, :] = split(w)
+        return 0
+    lax.fori_loop(0, lines // 2, update_rows, 0)
     for a in (0, 1):
         for k in (0, -1, 1, 2):
             d = 1 if k in (0, -1) else -1
@@ -582,9 +602,10 @@
     shape = lambda *s: jax.ShapeDtypeStruct(s, F32)
     vmem = lambda *s: pltpu.VMEM(s, F32)
     return pl.pallas_call(exchange_kernel,
-        out_shape=(shape(count, count), shape(rows, count), shape(cols, count), shape(lines, cells, cols)),
+        out_shape=(jax.ShapeDtypeStruct((rows, count), BF16), jax.ShapeDtypeStruct((rows, count), BF16), shape(cols, count),
+                   shape(lines, cells, cols)),
         in_specs=[hbm, v, v, v, v],
-        out_specs=(v, v, v, hbm),
+        out_specs=(v, v, hbm, hbm),
         scratch_shapes=[
             vmem(lines + 2, cells, cols + 2 * cells), pltpu.VMEM((cols, count), BF16), pltpu.VMEM((cols, count), BF16),
             vmem(16, count), vmem(lines, 4, cells, cells), vmem(cols // cells, 8, cells), vmem(cols // cells + 2, cells, cells),
@@ -592,8 +613,8 @@
             vmem(lines, cells, count), vmem(RING, cells, count), vmem(RING, cells, count),
             vmem(2, cells // 2, count), vmem(2, cells, count),
             vmem(count, count), vmem(half, count), vmem(2, 3, p1, half), vmem(2, 3, p2, half), vmem(2, RING, p2, half),
-            vmem(count, count),
-            pltpu.SemaphoreType.DMA((lines,)), pltpu.SemaphoreType.DMA((lines,)),
+            vmem(count, count), vmem(count, count), vmem(rows, count),
+            pltpu.SemaphoreType.DMA((lines,)), pltpu.SemaphoreType.DMA((lines,)), pltpu.SemaphoreType.DMA,
             pltpu.SemaphoreType.DMA((100,)), pltpu.SemaphoreType.DMA((100,))],
         compiler_params=pltpu.CompilerParams(vmem_limit_bytes=62 << 20, collective_id=0, has_side_effects=True),
         cost_estimate=pl.CostEstimate(flops=12 * 10**9, bytes_accessed=28 << 20, transcendentals=0),
@@ -601,8 +622,8 @@
 
 
 def body(prior, vel_first, vel_second, obs_cell, obs_noise):
-    s_inv, g_rows, g_cols, field = exchange(prior, vel_first, vel_second, obs_cell.T, obs_noise[None])
-    return finish(field.reshape(prior.shape), g_rows, s_inv, g_cols, tile=512)
+    w_high, w_low, g_cols, field = exchange(prior, vel_first, vel_second, obs_cell.T, obs_noise[None])
+    return finish(field.reshape(prior.shape), w_high, w_low, g_cols)
 
 
 def solution(mesh):

time: 135 us -> 122 us (0.904)
  the two profiles are of different devices: /device:TPU:1 before, /device:TPU:0 now
where the time goes in v4:
time: 122 us
  Pallas kernels  122 us (100%)
    pallas_call x1, Pallas kernels, exchange(): pl.pallas_call(exchange_kernel, out_shape=(jax.ShapeDtypeStruct((rows, co...  109 us
    pallas_call x1, Pallas kernels, finish(): pl.pallas_call(fin_kernel, grid=(cols // tile,), out_shape=jax.ShapeDtype...  12.2 us

profile of v4, /device:TPU:0, one launch (start us, length us, event | category | flops | bytes accessed | tf_op | source)
XLA Modules:
  0.0 121.7 jit_solution(6730831233409823229)
XLA Ops:
  0.0 109.5 %shard_map.55 = (bf16[1024,512]{1,0:T(8,128)(2,1)}, bf16[1024,512]{1,0:T(8,128)(2,1)}, f32[2048,512]{1,0:T(8,128)}, f32[8,128,2048]{2,1,0:T(8,128)}) custom-call(f32[8,128,2048]{2,1,0:T(8,128)} %bitcast.4, f32[128,128]{1,0:T(8,128)} %velf_ref.1, f32[128,128]{1,0:T(8,128)} %vels_ref.1, s32[2,512]{1,0:T(2,128)} %bitcast.5, f32[1,512]{1,0:T(1,128)} %bitcast.6), custom_call_target="tpu_custom_call" | custom-call | flops 12000000000 | bytes 29360128 | tf_op jit(solution)/shard_map/pallas_call | solution.py:604
  109.5 12.2 %shard_map.56 = f32[1024,2048]{1,0:T(8,128)} custom-call(f32[1024,2048]{1,0:T(8,128)} %bitcast.7, bf16[1024,512]{1,0:T(8,128)(2,1)} %get-tuple-element.10.wh_ref, bf16[1024,512]{1,0:T(8,128)(2,1)} %get-tuple-element.11.wlo_ref, f32[2048,512]{1,0:T(8,128)} %get-tuple-element.12.gc_ref), custom_call_target="tpu_custom_call" | custom-call | flops 8000000000 | bytes 25165824 | tf_op jit(solution)/shard_map/pallas_call | solution.py:165

commit v5 on v4

--- a/solution.py
+++ b/solution.py
@@ -193,6 +193,8 @@
             upd = jnp.dot(col, r, precision=HI, preferred_element_type=F32)
             o_ref[:, here] = -upd if j == k else o_ref[:, here] - upd
             o_ref[own, here] = r
+    for hook in hooks.get((nb, 0), ()):
+        hook()
 
 
 def pivot(a, steps):
@@ -562,7 +564,7 @@
         forecast_lines(0, 1)
         forecast_lines(lines - 1, lines)
 
-    hooks = {(0, 2): [p1], (1, 1): [edge_lines, p2], (1, 3): [p3, relays(0)], (2, 2): [p4, relays(-1, 1)], (3, 1): [relays(2)]}
+    hooks = {(1, 2): [p1], (2, 1): [p2], (3, 0): [p3, relays(0)], (3, 3): [p4, relays(-1)], (4, 0): [edge_lines, relays(1, 2)]}
 
     arrive("s_back", s_out.at[pl.ds(other, half), :], partner)
     invert_in(s_out, noise_ref, sinv_ref, hooks)

time: 122 us -> 119 us (0.975)
  the two profiles are of different devices: /device:TPU:0 before, /device:TPU:1 now
where the time goes in v5:
time: 119 us
  Pallas kernels  119 us (100%)
    pallas_call x1, Pallas kernels, exchange(): pl.pallas_call(exchange_kernel, out_shape=(jax.ShapeDtypeStruct((rows, co...  107 us
    pallas_call x1, Pallas kernels, finish(): pl.pallas_call(fin_kernel, grid=(cols // tile,), out_shape=jax.ShapeDtype...  12.2 us

profile of v5, /device:TPU:1, one launch (start us, length us, event | category | flops | bytes accessed | tf_op | source)
XLA Modules:
  0.0 119.0 jit_solution(6688424499464737513)
XLA Ops:
  0.0 106.8 %shard_map.55 = (bf16[1024,512]{1,0:T(8,128)(2,1)}, bf16[1024,512]{1,0:T(8,128)(2,1)}, f32[2048,512]{1,0:T(8,128)}, f32[8,128,2048]{2,1,0:T(8,128)}) custom-call(f32[8,128,2048]{2,1,0:T(8,128)} %bitcast.4, f32[128,128]{1,0:T(8,128)} %velf_ref.1, f32[128,128]{1,0:T(8,128)} %vels_ref.1, s32[2,512]{1,0:T(2,128)} %bitcast.5, f32[1,512]{1,0:T(1,128)} %bitcast.6), custom_call_target="tpu_custom_call" | custom-call | flops 12000000000 | bytes 29360128 | tf_op jit(solution)/shard_map/pallas_call | solution.py:606
  106.8 12.2 %shard_map.56 = f32[1024,2048]{1,0:T(8,128)} custom-call(f32[1024,2048]{1,0:T(8,128)} %bitcast.7, bf16[1024,512]{1,0:T(8,128)(2,1)} %get-tuple-element.10.wh_ref, bf16[1024,512]{1,0:T(8,128)(2,1)} %get-tuple-element.11.wlo_ref, f32[2048,512]{1,0:T(8,128)} %get-tuple-element.12.gc_ref), custom_call_target="tpu_custom_call" | custom-call | flops 8000000000 | bytes 25165824 | tf_op jit(solution)/shard_map/pallas_call | solution.py:165

commit v6 on v5

--- a/solution.py
+++ b/solution.py
@@ -564,7 +564,8 @@
         forecast_lines(0, 1)
         forecast_lines(lines - 1, lines)
 
-    hooks = {(1, 2): [p1], (2, 1): [p2], (3, 0): [p3, relays(0)], (3, 3): [p4, relays(-1)], (4, 0): [edge_lines, relays(1, 2)]}
+    hooks = {(1, 2): [p1], (2, 1): [p2], (3, 0): [p3, relays(0)], (3, 3): [p4, relays(-1)],
+             (4, 0): [relays(1), edge_lines, relays(2)]}
 
     arrive("s_back", s_out.at[pl.ds(other, half), :], partner)
     invert_in(s_out, noise_ref, sinv_ref, hooks)

time: 119 us -> 118 us (level); the launches traced: 119 us -> 117 us
  Pallas kernels: 119 us -> 117 us
    pallas_call x1, Pallas kernels: 107 us -> 105 us  [exchange(): pl.pallas_call(exchange_kernel, out_shape=(jax.ShapeDtypeStruct((rows, co...]
where the time goes in v6:
time: 118 us; the launch traced here: 117 us
  Pallas kernels  117 us (99%)
    pallas_call x1, Pallas kernels, exchange(): pl.pallas_call(exchange_kernel, out_shape=(jax.ShapeDtypeStruct((rows, co...  105 us
    pallas_call x1, Pallas kernels, finish(): pl.pallas_call(fin_kernel, grid=(cols // tile,), out_shape=jax.ShapeDtype...  12.2 us

profile of v6, /device:TPU:1, one launch (start us, length us, event | category | flops | bytes accessed | tf_op | source)
XLA Modules:
  0.0 116.8 jit_solution(12768155068681261072)
XLA Ops:
  0.0 104.6 %shard_map.55 = (bf16[1024,512]{1,0:T(8,128)(2,1)}, bf16[1024,512]{1,0:T(8,128)(2,1)}, f32[2048,512]{1,0:T(8,128)}, f32[8,128,2048]{2,1,0:T(8,128)}) custom-call(f32[8,128,2048]{2,1,0:T(8,128)} %bitcast.4, f32[128,128]{1,0:T(8,128)} %velf_ref.1, f32[128,128]{1,0:T(8,128)} %vels_ref.1, s32[2,512]{1,0:T(2,128)} %bitcast.5, f32[1,512]{1,0:T(1,128)} %bitcast.6), custom_call_target="tpu_custom_call" | custom-call | flops 12000000000 | bytes 29360128 | tf_op jit(solution)/shard_map/pallas_call | solution.py:607
  104.6 12.2 %shard_map.56 = f32[1024,2048]{1,0:T(8,128)} custom-call(f32[1024,2048]{1,0:T(8,128)} %bitcast.7, bf16[1024,512]{1,0:T(8,128)(2,1)} %get-tuple-element.10.wh_ref, bf16[1024,512]{1,0:T(8,128)(2,1)} %get-tuple-element.11.wlo_ref, f32[2048,512]{1,0:T(8,128)} %get-tuple-element.12.gc_ref), custom_call_target="tpu_custom_call" | custom-call | flops 8000000000 | bytes 25165824 | tf_op jit(solution)/shard_map/pallas_call | solution.py:165
